TPU v7x, 256 devices: a whole 4x4x8 slice. The times are simulated.
256 devices in a mesh: gx: 4 (over z_hi), gy: 16 (over x, z_lo, core), gz: 4 (over y).
Axes of the slice: x: 4, y: 4, z: 8 (z_hi: 4, z_lo: 2; z = z_hi * 2 + z_lo), core: 2. Of those that a mesh axis runs over, the one named last changes fastest.
Arguments:
- old_fields: float32 [2, 32, 64, 16, 1024], P(None, 'gy', 'gz', None, 'gx'), may hold values from -6 to 6
- old_coef: bfloat16 [4, 32, 64, 16, 1024], P(None, 'gy', 'gz', None, 'gx'), may hold values from 0.25 to 4
- held_slabs: int32 [32, 4, 4], P('gy', 'gz', 'gx'), may hold values from 0 to 24, as said below
Outputs:
- solution: float32 [64, 384, 1024], P('gz', 'gy', 'gx')
- residual: float32 [64, 384, 1024], P('gz', 'gy', 'gx')
Inputs may be any that keep to these rules, and one draw needn't show every extreme that they name: `held_slabs`: in every column of bricks and for every p below 8, rows 4p to 4p + 3 hold the old slabs 3p, 3p + 1, 3p + 2 once each and one entry 24, which marks an empty slot.
All inputs are finite; a program needn't handle non-finite values.
Results may differ from a plain program's by a relative error of at most 0.0003.
Values may be sent and summed in bfloat16 or wider, within the bound.
A program may use at most 64 MiB of HBM per device.

v0:
```python
import jax
import jax.numpy as jnp
from jax import lax
from jax.sharding import PartitionSpec as P

SWEEPS = 4


def from_partner(x, axis, distance):
    return lax.ppermute(x, axis, [(i, i ^ 1 << distance) for i in range(lax.axis_size(axis))])


def passed_along(value, axis, steps):
    count = lax.axis_size(axis)
    pairs = [(source, (source + steps) % count) for source in range(count)]
    return lax.ppermute(value, axis, pairs)


def extended(cells, sides, width):
    for axis, dim in sides:
        count = lax.axis_size(axis)
        head = lax.slice_in_dim(cells, 0, width, axis=dim)
        tail = lax.slice_in_dim(cells, cells.shape[dim] - width, cells.shape[dim], axis=dim)
        cells = jnp.concatenate(
            [
                lax.ppermute(tail, axis, [(i, (i + 1) % count) for i in range(count)]),
                cells,
                lax.ppermute(head, axis, [((i + 1) % count, i) for i in range(count)]),
            ],
            axis=dim,
        )
    return cells


def chebyshev_weights(count):
    low_bound = 0.25
    high_bound = 2.0
    centre_value = 0.5 * (high_bound + low_bound)
    half_width = 0.5 * (high_bound - low_bound)
    ratio_value = centre_value / half_width
    damping = 1.0 / ratio_value
    first_list = [0.0]
    second_list = [1.0 / centre_value]
    for step_index in range(1, count):
        damping_next = 1.0 / (2.0 * ratio_value - damping)
        first_list.append(damping_next * damping)
        second_list.append(2.0 * damping_next / half_width)
        damping = damping_next
    return (first_list, second_list)


def pick_slab(slot_data, slot_ids, target):
    chosen = jnp.zeros_like(slot_data[0])
    for data_piece, slab_id in zip(slot_data, slot_ids):
        chosen = jnp.where(slab_id == target, data_piece, chosen)
    return chosen


def apply_box(field_ext, face_terms):
    cell_alpha, beta_x, upper_x, beta_y, upper_y, beta_z, upper_z = face_terms
    centre = field_ext[1:-1, 1:-1, 1:-1]
    result = cell_alpha * centre
    result = (
        result
        + beta_x * (centre - field_ext[1:-1, 1:-1, :-2])
        + upper_x * (centre - field_ext[1:-1, 1:-1, 2:])
    )
    result = (
        result
        + beta_y * (centre - field_ext[1:-1, :-2, 1:-1])
        + upper_y * (centre - field_ext[1:-1, 2:, 1:-1])
    )
    result = (
        result
        + beta_z * (centre - field_ext[:-2, 1:-1, 1:-1])
        + upper_z * (centre - field_ext[2:, 1:-1, 1:-1])
    )
    return result


def inverse_diagonal(face_terms):
    cell_alpha, beta_x, upper_x, beta_y, upper_y, beta_z, upper_z = face_terms
    return 1.0 / (cell_alpha + beta_x + upper_x + beta_y + upper_y + beta_z + upper_z)


def local(old_fields, old_coef, held_slabs):
    group_index = lax.axis_index("gy")
    pair_first = 3 * (group_index // 2)
    own_half = group_index % 2
    unit_rows = old_fields.shape[3] // 2
    brick_rows = 3 * unit_rows
    own_ids = held_slabs[:, 0, 0]
    partner_fields, partner_ids = from_partner((old_fields, own_ids.astype(jnp.float32)), "gy", 0)
    partner_coef = from_partner(old_coef, "gy", 0)
    field_slots = [old_fields[:, 0], old_fields[:, 1], partner_fields[:, 0], partner_fields[:, 1]]
    coef_slots = [old_coef[:, 0], old_coef[:, 1], partner_coef[:, 0], partner_coef[:, 1]]
    slot_ids = [
        own_ids[0].astype(jnp.float32),
        own_ids[1].astype(jnp.float32),
        partner_ids[0],
        partner_ids[1],
    ]
    targets = [(pair_first + offset).astype(jnp.float32) for offset in range(3)]
    region_fields = jnp.concatenate(
        [pick_slab(field_slots, slot_ids, target) for target in targets], axis=2
    )
    region_coef = jnp.concatenate(
        [pick_slab(coef_slots, slot_ids, target) for target in targets], axis=2
    )
    grid_fields = lax.dynamic_slice_in_dim(region_fields, own_half * brick_rows, brick_rows, 2)
    grid_coef = lax.dynamic_slice_in_dim(region_coef, own_half * brick_rows, brick_rows, 2)
    solution = grid_fields[0]
    rhs_field = grid_fields[1]
    first_list, second_list = chebyshev_weights(SWEEPS)
    rim_x = passed_along(grid_coef[1][:, :, :1], "gx", -1)
    rim_y = passed_along(grid_coef[2][:, :1, :], "gy", -1)
    rim_z = passed_along(grid_coef[3][:1], "gz", -1)
    upper_x = jnp.concatenate([grid_coef[1][:, :, 1:], rim_x], axis=2)
    upper_y = jnp.concatenate([grid_coef[2][:, 1:, :], rim_y], axis=1)
    upper_z = jnp.concatenate([grid_coef[3][1:], rim_z], axis=0)
    face_terms = tuple(
        (
            member.astype(jnp.float32)
            for member in (
                grid_coef[0],
                grid_coef[1],
                upper_x,
                grid_coef[2],
                upper_y,
                grid_coef[3],
                upper_z,
            )
        )
    )
    inverse = inverse_diagonal(face_terms)

    def extend(field):
        return extended(field, (("gx", 2), ("gy", 1), ("gz", 0)), 1)

    residual = rhs_field - apply_box(extend(solution), face_terms)
    direction = jnp.zeros_like(solution)
    for sweep_index in range(SWEEPS):
        direction = first_list[sweep_index] * direction + second_list[sweep_index] * (
            inverse * residual
        )
        solution = solution + direction
        residual = residual - apply_box(extend(direction), face_terms)
    return (solution, residual)


def solution(mesh):
    in_specs = (
        P(None, "gy", "gz", None, "gx"),
        P(None, "gy", "gz", None, "gx"),
        P("gy", "gz", "gx"),
    )
    out_specs = (P("gz", "gy", "gx"), P("gz", "gy", "gx"))
    return jax.shard_map(local, mesh=mesh, in_specs=in_specs, out_specs=out_specs, check_vma=False)
```

profile of v0, /device:TPU:24, one launch (start us, length us, event | category | flops | bytes accessed | tf_op | source)
XLA Modules:
  0.0 148.5 jit_solution(8658779896572516821)
XLA Ops:
  0.6 2.4 %copy.5 = f32[2,2,16,16,256]{4,3,2,0,1:T(8,128)} copy(f32[2,2,16,16,256]{4,3,2,1,0:T(8,128)} %param.3) | data formatting | bytes 2097152 | tf_op args[0]
  14.5 3.3 %collective-permute-start.6 = (f32[16,24,1]{2,1,0:T(8,128)S(1)}, f32[16,24,1]{2,1,0:T(8,128)S(1)}, u32[]{:S(2)}, u32[]{:S(2)}) collective-permute-start(f32[16,24,1]{2,1,0:T(8,128)S(1)} %get-tuple-element.46), channel_id=1, source_target_pairs={{0,64},{64,128},{128,192},{192,0},{1,65},{65,129},{129,193},{193,1... | collective-permute-start | bytes 4616 | tf_op jit(solution)/shard_map/ppermute | solution.py:26
  17.9 3.1 %collective-permute-start.7 = (f32[16,24,1]{2,1,0:T(8,128)S(1)}, f32[16,24,1]{2,1,0:T(8,128)S(1)}, u32[]{:S(2)}, u32[]{:S(2)}) collective-permute-start(f32[16,24,1]{2,1,0:T(8,128)S(1)} %get-tuple-element.47), channel_id=1, source_target_pairs={{64,0},{128,64},{192,128},{0,192},{65,1},{129,65},{193,129},{1,193... | collective-permute-start | bytes 4616 | tf_op jit(solution)/shard_map/ppermute | solution.py:28
  22.2 5.7 %collective-permute-done.6 = f32[16,24,1]{2,1,0:T(8,128)S(1)} collective-permute-done((f32[16,24,1]{2,1,0:T(8,128)S(1)}, f32[16,24,1]{2,1,0:T(8,128)S(1)}, u32[]{:S(2)}, u32[]{:S(2)}) %collective-permute-start.6) | collective-permute-done | bytes 1568 | tf_op jit(solution)/shard_map/ppermute | solution.py:26
  27.9 3.8 %collective-permute-done.7 = f32[16,24,1]{2,1,0:T(8,128)S(1)} collective-permute-done((f32[16,24,1]{2,1,0:T(8,128)S(1)}, f32[16,24,1]{2,1,0:T(8,128)S(1)}, u32[]{:S(2)}, u32[]{:S(2)}) %collective-permute-start.7) | collective-permute-done | bytes 1568 | tf_op jit(solution)/shard_map/ppermute | solution.py:28
  32.1 3.8 %collective-permute-start.9 = (f32[16,1,258]{2,1,0:T(1,128)S(1)}, f32[16,1,258]{2,1,0:T(1,128)S(1)}, u32[]{:S(2)}, u32[]{:S(2)}) collective-permute-start(f32[16,1,258]{2,1,0:T(1,128)S(1)} %get-tuple-element.37), channel_id=1, source_target_pairs={{4,0},{8,4},{12,8},{16,12},{20,16},{24,20},{28,24},{32,28},{36,32}... | collective-permute-start | bytes 49544 | tf_op jit(solution)/shard_map/ppermute | solution.py:28
  36.8 2.8 %collective-permute-start.3 = (bf16[16,24,1]{2,1,0:T(8,128)(2,1)S(1)}, bf16[16,24,1]{2,1,0:T(8,128)(2,1)S(1)}, u32[]{:S(2)}, u32[]{:S(2)}) collective-permute-start(bf16[16,24,1]{2,1,0:T(8,128)(2,1)S(1)} %slice.396), channel_id=1, source_target_pairs={{0,192},{64,0},{128,64},{192,128},{1,193},{65,1},{129,65},{193,129... | collective-permute-start | bytes 2312 | tf_op jit(solution)/shard_map/ppermute | solution.py:16
  39.7 2.6 %collective-permute-start.10 = (f32[1,26,258]{2,1,0:T(8,128)S(1)}, f32[1,26,258]{2,1,0:T(8,128)S(1)}, u32[]{:S(2)}, u32[]{:S(2)}) collective-permute-start(f32[1,26,258]{2,1,0:T(8,128)S(1)} %get-tuple-element.24), channel_id=1, source_target_pairs={{0,1},{1,2},{2,3},{3,0},{4,5},{5,6},{6,7},{7,4},{8,9},{9,10},{10,1... | collective-permute-start | bytes 80504 | tf_op jit(solution)/shard_map/ppermute | solution.py:26
  44.3 3.3 %collective-permute-done.11 = f32[1,26,258]{2,1,0:T(8,128)S(1)} collective-permute-done((f32[1,26,258]{2,1,0:T(8,128)S(1)}, f32[1,26,258]{2,1,0:T(8,128)S(1)}, u32[]{:S(2)}, u32[]{:S(2)}) %collective-permute-start.11) | collective-permute-done | bytes 26864 | tf_op jit(solution)/shard_map/ppermute | solution.py:28
  50.5 2.5 %collective-permute-start.13 = (f32[16,24,1]{2,1,0:T(8,128)S(1)}, f32[16,24,1]{2,1,0:T(8,128)S(1)}, u32[]{:S(2)}, u32[]{:S(2)}) collective-permute-start(f32[16,24,1]{2,1,0:T(8,128)S(1)} %get-tuple-element.45), channel_id=1, source_target_pairs={{64,0},{128,64},{192,128},{0,192},{65,1},{129,65},{193,129},{1,193... | collective-permute-start | bytes 4616 | tf_op jit(solution)/shard_map/ppermute | solution.py:28
  52.9 5.6 %collective-permute-done.12 = f32[16,24,1]{2,1,0:T(8,128)S(1)} collective-permute-done((f32[16,24,1]{2,1,0:T(8,128)S(1)}, f32[16,24,1]{2,1,0:T(8,128)S(1)}, u32[]{:S(2)}, u32[]{:S(2)}) %collective-permute-start.12) | collective-permute-done | bytes 1568 | tf_op jit(solution)/shard_map/ppermute | solution.py:26
  58.5 2.1 %collective-permute-done.13 = f32[16,24,1]{2,1,0:T(8,128)S(1)} collective-permute-done((f32[16,24,1]{2,1,0:T(8,128)S(1)}, f32[16,24,1]{2,1,0:T(8,128)S(1)}, u32[]{:S(2)}, u32[]{:S(2)}) %collective-permute-start.13) | collective-permute-done | bytes 1568 | tf_op jit(solution)/shard_map/ppermute | solution.py:28
  60.9 3.8 %collective-permute-start.15 = (f32[16,1,258]{2,1,0:T(1,128)S(1)}, f32[16,1,258]{2,1,0:T(1,128)S(1)}, u32[]{:S(2)}, u32[]{:S(2)}) collective-permute-start(f32[16,1,258]{2,1,0:T(1,128)S(1)} %get-tuple-element.33), channel_id=1, source_target_pairs={{4,0},{8,4},{12,8},{16,12},{20,16},{24,20},{28,24},{32,28},{36,32}... | collective-permute-start | bytes 49544 | tf_op jit(solution)/shard_map/ppermute | solution.py:28
  68.5 2.1 %collective-permute-done.16 = f32[1,26,258]{2,1,0:T(8,128)S(1)} collective-permute-done((f32[1,26,258]{2,1,0:T(8,128)S(1)}, f32[1,26,258]{2,1,0:T(8,128)S(1)}, u32[]{:S(2)}, u32[]{:S(2)}) %collective-permute-start.16) | collective-permute-done | bytes 26864 | tf_op jit(solution)/shard_map/ppermute | solution.py:26
  70.6 2.9 %collective-permute-done.17 = f32[1,26,258]{2,1,0:T(8,128)S(1)} collective-permute-done((f32[1,26,258]{2,1,0:T(8,128)S(1)}, f32[1,26,258]{2,1,0:T(8,128)S(1)}, u32[]{:S(2)}, u32[]{:S(2)}) %collective-permute-start.17) | collective-permute-done | bytes 26864 | tf_op jit(solution)/shard_map/ppermute | solution.py:28
  74.4 2.6 %collective-permute-start.18 = (f32[16,24,1]{2,1,0:T(8,128)S(1)}, f32[16,24,1]{2,1,0:T(8,128)S(1)}, u32[]{:S(2)}, u32[]{:S(2)}) collective-permute-start(f32[16,24,1]{2,1,0:T(8,128)S(1)} %get-tuple-element.42), channel_id=1, source_target_pairs={{0,64},{64,128},{128,192},{192,0},{1,65},{65,129},{129,193},{193,1... | collective-permute-start | bytes 4616 | tf_op jit(solution)/shard_map/ppermute | solution.py:26
  78.7 7.3 %collective-permute-done.18 = f32[16,24,1]{2,1,0:T(8,128)S(1)} collective-permute-done((f32[16,24,1]{2,1,0:T(8,128)S(1)}, f32[16,24,1]{2,1,0:T(8,128)S(1)}, u32[]{:S(2)}, u32[]{:S(2)}) %collective-permute-start.18) | collective-permute-done | bytes 1568 | tf_op jit(solution)/shard_map/ppermute | solution.py:26
  87.1 3.8 %collective-permute-start.21 = (f32[16,1,258]{2,1,0:T(1,128)S(1)}, f32[16,1,258]{2,1,0:T(1,128)S(1)}, u32[]{:S(2)}, u32[]{:S(2)}) collective-permute-start(f32[16,1,258]{2,1,0:T(1,128)S(1)} %get-tuple-element.31), channel_id=1, source_target_pairs={{4,0},{8,4},{12,8},{16,12},{20,16},{24,20},{28,24},{32,28},{36,32}... | collective-permute-start | bytes 49544 | tf_op jit(solution)/shard_map/ppermute | solution.py:28
  100.6 2.9 %collective-permute-start.25 = (f32[16,24,1]{2,1,0:T(8,128)S(1)}, f32[16,24,1]{2,1,0:T(8,128)S(1)}, u32[]{:S(2)}, u32[]{:S(2)}) collective-permute-start(f32[16,24,1]{2,1,0:T(8,128)S(1)} %get-tuple-element.41), channel_id=1, source_target_pairs={{64,0},{128,64},{192,128},{0,192},{65,1},{129,65},{193,129},{1,193... | collective-permute-start | bytes 4616 | tf_op jit(solution)/shard_map/ppermute | solution.py:28
  103.5 6.4 %collective-permute-done.24 = f32[16,24,1]{2,1,0:T(8,128)S(1)} collective-permute-done((f32[16,24,1]{2,1,0:T(8,128)S(1)}, f32[16,24,1]{2,1,0:T(8,128)S(1)}, u32[]{:S(2)}, u32[]{:S(2)}) %collective-permute-start.24) | collective-permute-done | bytes 1568 | tf_op jit(solution)/shard_map/ppermute | solution.py:26
  110.6 3.8 %collective-permute-start.27 = (f32[16,1,258]{2,1,0:T(1,128)S(1)}, f32[16,1,258]{2,1,0:T(1,128)S(1)}, u32[]{:S(2)}, u32[]{:S(2)}) collective-permute-start(f32[16,1,258]{2,1,0:T(1,128)S(1)} %get-tuple-element.29), channel_id=1, source_target_pairs={{4,0},{8,4},{12,8},{16,12},{20,16},{24,20},{28,24},{32,28},{36,32}... | collective-permute-start | bytes 49544 | tf_op jit(solution)/shard_map/ppermute | solution.py:28
  122.5 2.6 %collective-permute-start.30 = (f32[16,24,1]{2,1,0:T(8,128)S(1)}, f32[16,24,1]{2,1,0:T(8,128)S(1)}, u32[]{:S(2)}, u32[]{:S(2)}) collective-permute-start(f32[16,24,1]{2,1,0:T(8,128)S(1)} %get-tuple-element.38), channel_id=1, source_target_pairs={{0,64},{64,128},{128,192},{192,0},{1,65},{65,129},{129,193},{193,1... | collective-permute-start | bytes 4616 | tf_op jit(solution)/shard_map/ppermute | solution.py:26
  126.7 7.0 %collective-permute-done.30 = f32[16,24,1]{2,1,0:T(8,128)S(1)} collective-permute-done((f32[16,24,1]{2,1,0:T(8,128)S(1)}, f32[16,24,1]{2,1,0:T(8,128)S(1)}, u32[]{:S(2)}, u32[]{:S(2)}) %collective-permute-start.30) | collective-permute-done | bytes 1568 | tf_op jit(solution)/shard_map/ppermute | solution.py:26
  135.8 3.8 %collective-permute-start.33 = (f32[16,1,258]{2,1,0:T(1,128)S(1)}, f32[16,1,258]{2,1,0:T(1,128)S(1)}, u32[]{:S(2)}, u32[]{:S(2)}) collective-permute-start(f32[16,1,258]{2,1,0:T(1,128)S(1)} %get-tuple-element.27), channel_id=1, source_target_pairs={{4,0},{8,4},{12,8},{16,12},{20,16},{24,20},{28,24},{32,28},{36,32}... | collective-permute-start | bytes 49544 | tf_op jit(solution)/shard_map/ppermute | solution.py:28
  (94 shorter events, 52.0 us)
Async XLA Ops:
  3.1 8.1 %collective-permute-start.1 = (f32[2,2,16,16,256]{4,3,2,0,1:T(8,128)}, f32[2,2,16,16,256]{4,3,2,0,1:T(8,128)}, u32[]{:S(2)}, u32[]{:S(2)}) collective-permute-start(f32[2,2,16,16,256]{4,3,2,0,1:T(8,128)} %copy.5), channel_id=1, source_target_pairs={{0,4},{4,0},{8,12},{12,8},{16,20},{20,16},{24,28},{28,24},{32,36},... | collective-permute-start | bytes 3145736 | tf_op jit(solution)/shard_map/ppermute | solution.py:10
  4.7 16.3 %collective-permute-start.2 = (bf16[4,2,16,16,256]{4,3,2,0,1:T(8,128)(2,1)}, bf16[4,2,16,16,256]{4,3,2,0,1:T(8,128)(2,1)S(1)}, u32[]{:S(2)}, u32[]{:S(2)}) collective-permute-start(bf16[4,2,16,16,256]{4,3,2,0,1:T(8,128)(2,1)} %copy.8), channel_id=1, source_target_pairs={{0,4},{4,0},{8,12},{12,8},{16,20},{20,16},{24,28},{28,24},{32,36},... | collective-permute-start | bytes 3145736 | tf_op jit(solution)/shard_map/ppermute | solution.py:10
  14.5 13.4 %collective-permute-start.6 = (f32[16,24,1]{2,1,0:T(8,128)S(1)}, f32[16,24,1]{2,1,0:T(8,128)S(1)}, u32[]{:S(2)}, u32[]{:S(2)}) collective-permute-start(f32[16,24,1]{2,1,0:T(8,128)S(1)} %get-tuple-element.46), channel_id=1, source_target_pairs={{0,64},{64,128},{128,192},{192,0},{1,65},{65,129},{129,193},{193,1... | collective-permute-start | bytes 4616 | tf_op jit(solution)/shard_map/ppermute | solution.py:26
  17.9 13.9 %collective-permute-start.7 = (f32[16,24,1]{2,1,0:T(8,128)S(1)}, f32[16,24,1]{2,1,0:T(8,128)S(1)}, u32[]{:S(2)}, u32[]{:S(2)}) collective-permute-start(f32[16,24,1]{2,1,0:T(8,128)S(1)} %get-tuple-element.47), channel_id=1, source_target_pairs={{64,0},{128,64},{192,128},{0,192},{65,1},{129,65},{193,129},{1,193... | collective-permute-start | bytes 4616 | tf_op jit(solution)/shard_map/ppermute | solution.py:28
  32.0 7.7 %collective-permute-start.8 = (f32[16,1,258]{2,1,0:T(1,128)S(1)}, f32[16,1,258]{2,1,0:T(1,128)S(1)}, u32[]{:S(2)}, u32[]{:S(2)}) collective-permute-start(f32[16,1,258]{2,1,0:T(1,128)S(1)} %get-tuple-element.36), channel_id=1, source_target_pairs={{0,4},{4,8},{8,12},{12,16},{16,20},{20,24},{24,28},{28,32},{32,36}... | collective-permute-start | bytes 49544 | tf_op jit(solution)/shard_map/ppermute | solution.py:26
  32.1 7.6 %collective-permute-start.9 = (f32[16,1,258]{2,1,0:T(1,128)S(1)}, f32[16,1,258]{2,1,0:T(1,128)S(1)}, u32[]{:S(2)}, u32[]{:S(2)}) collective-permute-start(f32[16,1,258]{2,1,0:T(1,128)S(1)} %get-tuple-element.37), channel_id=1, source_target_pairs={{4,0},{8,4},{12,8},{16,12},{20,16},{24,20},{28,24},{32,28},{36,32}... | collective-permute-start | bytes 49544 | tf_op jit(solution)/shard_map/ppermute | solution.py:28
  35.9 8.4 %collective-permute-start.5 = (bf16[1,24,256]{2,1,0:T(8,128)(2,1)S(1)}, bf16[1,24,256]{2,1,0:T(8,128)(2,1)S(1)}, u32[]{:S(2)}, u32[]{:S(2)}) collective-permute-start(bf16[1,24,256]{2,1,0:T(8,128)(2,1)S(1)} %slice_bitcast_fusion.7), channel_id=1, source_target_pairs={{0,3},{1,0},{2,1},{3,2},{4,7},{5,4},{6,5},{7,6},{8,11},{9,8},{10,9... | collective-permute-start | bytes 36872 | tf_op jit(solution)/shard_map/ppermute | solution.py:16
  36.7 7.7 %collective-permute-start.4 = (bf16[16,1,256]{2,1,0:T(2,128)(2,1)S(1)}, bf16[16,1,256]{2,1,0:T(2,128)(2,1)S(1)}, u32[]{:S(2)}, u32[]{:S(2)}) collective-permute-start(bf16[16,1,256]{2,1,0:T(2,128)(2,1)S(1)} %slice.399), channel_id=1, source_target_pairs={{0,60},{4,0},{8,4},{12,8},{16,12},{20,16},{24,20},{28,24},{32,28},... | collective-permute-start | bytes 24584 | tf_op jit(solution)/shard_map/ppermute | solution.py:16
  36.8 7.6 %collective-permute-start.3 = (bf16[16,24,1]{2,1,0:T(8,128)(2,1)S(1)}, bf16[16,24,1]{2,1,0:T(8,128)(2,1)S(1)}, u32[]{:S(2)}, u32[]{:S(2)}) collective-permute-start(bf16[16,24,1]{2,1,0:T(8,128)(2,1)S(1)} %slice.396), channel_id=1, source_target_pairs={{0,192},{64,0},{128,64},{192,128},{1,193},{65,1},{129,65},{193,129... | collective-permute-start | bytes 2312 | tf_op jit(solution)/shard_map/ppermute | solution.py:16
  48.7 9.8 %collective-permute-start.12 = (f32[16,24,1]{2,1,0:T(8,128)S(1)}, f32[16,24,1]{2,1,0:T(8,128)S(1)}, u32[]{:S(2)}, u32[]{:S(2)}) collective-permute-start(f32[16,24,1]{2,1,0:T(8,128)S(1)} %get-tuple-element.44), channel_id=1, source_target_pairs={{0,64},{64,128},{128,192},{192,0},{1,65},{65,129},{129,193},{193,1... | collective-permute-start | bytes 4616 | tf_op jit(solution)/shard_map/ppermute | solution.py:26
  50.5 10.2 %collective-permute-start.13 = (f32[16,24,1]{2,1,0:T(8,128)S(1)}, f32[16,24,1]{2,1,0:T(8,128)S(1)}, u32[]{:S(2)}, u32[]{:S(2)}) collective-permute-start(f32[16,24,1]{2,1,0:T(8,128)S(1)} %get-tuple-element.45), channel_id=1, source_target_pairs={{64,0},{128,64},{192,128},{0,192},{65,1},{129,65},{193,129},{1,193... | collective-permute-start | bytes 4616 | tf_op jit(solution)/shard_map/ppermute | solution.py:28
  60.8 5.4 %collective-permute-start.14 = (f32[16,1,258]{2,1,0:T(1,128)S(1)}, f32[16,1,258]{2,1,0:T(1,128)S(1)}, u32[]{:S(2)}, u32[]{:S(2)}) collective-permute-start(f32[16,1,258]{2,1,0:T(1,128)S(1)} %get-tuple-element.32), channel_id=1, source_target_pairs={{0,4},{4,8},{8,12},{12,16},{16,20},{20,24},{24,28},{28,32},{32,36}... | collective-permute-start | bytes 49544 | tf_op jit(solution)/shard_map/ppermute | solution.py:26
  74.4 11.5 %collective-permute-start.18 = (f32[16,24,1]{2,1,0:T(8,128)S(1)}, f32[16,24,1]{2,1,0:T(8,128)S(1)}, u32[]{:S(2)}, u32[]{:S(2)}) collective-permute-start(f32[16,24,1]{2,1,0:T(8,128)S(1)} %get-tuple-element.42), channel_id=1, source_target_pairs={{0,64},{64,128},{128,192},{192,0},{1,65},{65,129},{129,193},{193,1... | collective-permute-start | bytes 4616 | tf_op jit(solution)/shard_map/ppermute | solution.py:26
  77.1 9.8 %collective-permute-start.19 = (f32[16,24,1]{2,1,0:T(8,128)S(1)}, f32[16,24,1]{2,1,0:T(8,128)S(1)}, u32[]{:S(2)}, u32[]{:S(2)}) collective-permute-start(f32[16,24,1]{2,1,0:T(8,128)S(1)} %get-tuple-element.43), channel_id=1, source_target_pairs={{64,0},{128,64},{192,128},{0,192},{65,1},{129,65},{193,129},{1,193... | collective-permute-start | bytes 4616 | tf_op jit(solution)/shard_map/ppermute | solution.py:28
  87.0 5.4 %collective-permute-start.20 = (f32[16,1,258]{2,1,0:T(1,128)S(1)}, f32[16,1,258]{2,1,0:T(1,128)S(1)}, u32[]{:S(2)}, u32[]{:S(2)}) collective-permute-start(f32[16,1,258]{2,1,0:T(1,128)S(1)} %get-tuple-element.30), channel_id=1, source_target_pairs={{0,4},{4,8},{8,12},{12,16},{16,20},{20,24},{24,28},{28,32},{32,36}... | collective-permute-start | bytes 49544 | tf_op jit(solution)/shard_map/ppermute | solution.py:26
  87.1 5.4 %collective-permute-start.21 = (f32[16,1,258]{2,1,0:T(1,128)S(1)}, f32[16,1,258]{2,1,0:T(1,128)S(1)}, u32[]{:S(2)}, u32[]{:S(2)}) collective-permute-start(f32[16,1,258]{2,1,0:T(1,128)S(1)} %get-tuple-element.31), channel_id=1, source_target_pairs={{4,0},{8,4},{12,8},{16,12},{20,16},{24,20},{28,24},{32,28},{36,32}... | collective-permute-start | bytes 49544 | tf_op jit(solution)/shard_map/ppermute | solution.py:28
  92.9 5.4 %collective-permute-start.23 = (f32[1,26,258]{2,1,0:T(8,128)S(1)}, f32[1,26,258]{2,1,0:T(8,128)S(1)}, u32[]{:S(2)}, u32[]{:S(2)}) collective-permute-start(f32[1,26,258]{2,1,0:T(8,128)S(1)} %get-tuple-element.21), channel_id=1, source_target_pairs={{1,0},{2,1},{3,2},{0,3},{5,4},{6,5},{7,6},{4,7},{9,8},{10,9},{11,1... | collective-permute-start | bytes 80504 | tf_op jit(solution)/shard_map/ppermute | solution.py:28
  99.3 10.7 %collective-permute-start.24 = (f32[16,24,1]{2,1,0:T(8,128)S(1)}, f32[16,24,1]{2,1,0:T(8,128)S(1)}, u32[]{:S(2)}, u32[]{:S(2)}) collective-permute-start(f32[16,24,1]{2,1,0:T(8,128)S(1)} %get-tuple-element.40), channel_id=1, source_target_pairs={{0,64},{64,128},{128,192},{192,0},{1,65},{65,129},{129,193},{193,1... | collective-permute-start | bytes 4616 | tf_op jit(solution)/shard_map/ppermute | solution.py:26
  100.6 9.7 %collective-permute-start.25 = (f32[16,24,1]{2,1,0:T(8,128)S(1)}, f32[16,24,1]{2,1,0:T(8,128)S(1)}, u32[]{:S(2)}, u32[]{:S(2)}) collective-permute-start(f32[16,24,1]{2,1,0:T(8,128)S(1)} %get-tuple-element.41), channel_id=1, source_target_pairs={{64,0},{128,64},{192,128},{0,192},{65,1},{129,65},{193,129},{1,193... | collective-permute-start | bytes 4616 | tf_op jit(solution)/shard_map/ppermute | solution.py:28
  110.5 5.4 %collective-permute-start.26 = (f32[16,1,258]{2,1,0:T(1,128)S(1)}, f32[16,1,258]{2,1,0:T(1,128)S(1)}, u32[]{:S(2)}, u32[]{:S(2)}) collective-permute-start(f32[16,1,258]{2,1,0:T(1,128)S(1)} %get-tuple-element.28), channel_id=1, source_target_pairs={{0,4},{4,8},{8,12},{12,16},{16,20},{20,24},{24,28},{28,32},{32,36}... | collective-permute-start | bytes 49544 | tf_op jit(solution)/shard_map/ppermute | solution.py:26
  122.5 11.3 %collective-permute-start.30 = (f32[16,24,1]{2,1,0:T(8,128)S(1)}, f32[16,24,1]{2,1,0:T(8,128)S(1)}, u32[]{:S(2)}, u32[]{:S(2)}) collective-permute-start(f32[16,24,1]{2,1,0:T(8,128)S(1)} %get-tuple-element.38), channel_id=1, source_target_pairs={{0,64},{64,128},{128,192},{192,0},{1,65},{65,129},{129,193},{193,1... | collective-permute-start | bytes 4616 | tf_op jit(solution)/shard_map/ppermute | solution.py:26
  125.1 10.4 %collective-permute-start.31 = (f32[16,24,1]{2,1,0:T(8,128)S(1)}, f32[16,24,1]{2,1,0:T(8,128)S(1)}, u32[]{:S(2)}, u32[]{:S(2)}) collective-permute-start(f32[16,24,1]{2,1,0:T(8,128)S(1)} %get-tuple-element.39), channel_id=1, source_target_pairs={{64,0},{128,64},{192,128},{0,192},{65,1},{129,65},{193,129},{1,193... | collective-permute-start | bytes 4616 | tf_op jit(solution)/shard_map/ppermute | solution.py:28
  135.7 5.4 %collective-permute-start.32 = (f32[16,1,258]{2,1,0:T(1,128)S(1)}, f32[16,1,258]{2,1,0:T(1,128)S(1)}, u32[]{:S(2)}, u32[]{:S(2)}) collective-permute-start(f32[16,1,258]{2,1,0:T(1,128)S(1)} %get-tuple-element.26), channel_id=1, source_target_pairs={{0,4},{4,8},{8,12},{12,16},{16,20},{20,24},{24,28},{28,32},{32,36}... | collective-permute-start | bytes 49544 | tf_op jit(solution)/shard_map/ppermute | solution.py:26
  135.8 5.4 %collective-permute-start.33 = (f32[16,1,258]{2,1,0:T(1,128)S(1)}, f32[16,1,258]{2,1,0:T(1,128)S(1)}, u32[]{:S(2)}, u32[]{:S(2)}) collective-permute-start(f32[16,1,258]{2,1,0:T(1,128)S(1)} %get-tuple-element.27), channel_id=1, source_target_pairs={{4,0},{8,4},{12,8},{16,12},{20,16},{24,20},{28,24},{32,28},{36,32}... | collective-permute-start | bytes 49544 | tf_op jit(solution)/shard_map/ppermute | solution.py:28
  (15 other events, 70.3 us)
where the time goes:
time: 149 us
  waiting for transfers between devices  66.6 us (45%)
  starting transfers between devices  58.2 us (39%)
  other arithmetic  12 us (8%)
  between operations  6.18 us (4%)
  local copies, waits for them, and re-layouts  5.5 us (4%)
    ppermute x15, waiting for transfers between devices, extended(): lax.ppermute(tail, axis, [(i, (i + 1) % count) for i in range(count)])  45.4 us
    ppermute x15, starting transfers between devices, extended(): lax.ppermute(head, axis, [((i + 1) % count, i) for i in range(count)])  37 us
    ppermute x15, waiting for transfers between devices, extended(): lax.ppermute(head, axis, [((i + 1) % count, i) for i in range(count)])  19.4 us
    ppermute x15, starting transfers between devices, extended(): lax.ppermute(tail, axis, [(i, (i + 1) % count) for i in range(count)])  16.9 us
    ppermute x3, starting transfers between devices, passed_along(): return lax.ppermute(value, axis, pairs)  3.67 us
    select_n x4, other arithmetic, pick_slab(): chosen = jnp.where(slab_id == target, data_piece, chosen)  3.63 us
    unnamed x8, local copies, waits for them, and re-layouts  3.52 us
  transfers between devices with their start and end apart: 36, of which 24 were waited for; matrix products, arithmetic and copies ran while one was open for 5% of the time, Pallas kernels for 0%

commit v1 on v0

v1 whole, which is shorter than its diff:
```python
import functools
import jax
import jax.numpy as jnp
from jax import lax
from jax.experimental import pallas as pl
from jax.experimental.pallas import tpu as pltpu
from jax.sharding import PartitionSpec as P

SWEEPS = 4
NZ = 16
NY = 24
NX = 256
ROWS = 8
LANES = 128
GROUPS = NY // ROWS
PLANES = 4
MESH = pl.DeviceIdType.MESH
F32 = jnp.float32
BF16 = jnp.bfloat16


def chebyshev_weights(count):
    low_bound = 0.25
    high_bound = 2.0
    centre_value = 0.5 * (high_bound + low_bound)
    half_width = 0.5 * (high_bound - low_bound)
    ratio_value = centre_value / half_width
    damping = 1.0 / ratio_value
    first_list = [0.0]
    second_list = [1.0 / centre_value]
    for step_index in range(1, count):
        damping_next = 1.0 / (2.0 * ratio_value - damping)
        first_list.append(damping_next * damping)
        second_list.append(2.0 * damping_next / half_width)
        damping = damping_next
    return first_list, second_list


FIRST, SECOND = chebyshev_weights(SWEEPS)


def ring(axis):
    count = lax.axis_size(axis)
    me = lax.axis_index(axis)
    low = {axis: lax.rem(me + count - 1, count)}
    high = {axis: lax.rem(me + 1, count)}
    return low, high


def kernel(
    fields_hbm, coef_hbm, held_ref, x_hbm, r_hbm,
    slots_f, slots_c, send_f, send_c, recv_f, recv_c,
    field, alpha, bx, by, bz, rhs, near, diag, scaled, total, resid,
    pack, face_y, halo_x, halo_y, rim_pack, rim_face, rim_x, rim_y,
    load_sem, pair_send, pair_recv, halo_send, halo_recv, rim_send, rim_recv, out_sem,
):
    loads_f = [pltpu.make_async_copy(fields_hbm.at[c], slots_f.at[c], load_sem.at[c]) for c in range(2)]
    loads_c = [pltpu.make_async_copy(coef_hbm.at[c], slots_c.at[c], load_sem.at[2 + c]) for c in range(4)]
    loads_f[0].start()
    for c in (1, 2, 3, 0):
        loads_c[c].start()
    loads_f[1].start()

    group = lax.axis_index("gy")
    half = lax.rem(group, 2)
    first_slab = 3 * (group // 2)
    partner = {"gy": group + 1 - 2 * half}
    x_low, x_high = ring("gx")
    y_low, y_high = ring("gy")
    z_low, z_high = ring("gz")

    barrier = pltpu.get_barrier_semaphore()
    for neighbour in (x_low, x_high, y_low, y_high, z_low, z_high):
        pl.semaphore_signal(barrier, inc=1, device_id=neighbour, device_id_type=MESH)

    id0 = held_ref[0, 0, 0]
    id1 = held_ref[1, 0, 0]
    mine = [first_slab + (3 * half + g) // 2 for g in range(GROUPS)]
    theirs = [first_slab + (3 * (1 - half) + g) // 2 for g in range(GROUPS)]
    my_part = [lax.rem(half + g, 2) for g in range(GROUPS)]
    their_part = [lax.rem(1 - half + g, 2) for g in range(GROUPS)]

    row = lax.broadcasted_iota(jnp.int32, (NY, LANES), 0)
    lane = lax.broadcasted_iota(jnp.int32, (NY, LANES), 1)
    lane8 = lax.broadcasted_iota(jnp.int32, (ROWS, LANES), 1)
    top_row = row == 0
    end_row = row == NY - 1
    first_lane = lane == 0
    last_lane = lane == LANES - 1

    def copy_to(source, target, send_sem, recv_sem, device):
        return pltpu.make_async_remote_copy(
            src_ref=source, dst_ref=target, send_sem=send_sem, recv_sem=recv_sem,
            device_id=device, device_id_type=MESH,
        )

    pair_f = [copy_to(send_f.at[c], recv_f.at[c], pair_send.at[c], pair_recv.at[c], partner) for c in range(2)]
    pair_c = [
        copy_to(send_c.at[c], recv_c.at[c], pair_send.at[2 + c], pair_recv.at[2 + c], partner) for c in range(4)
    ]

    def halo_copies(k):
        return [
            copy_to(pack.at[k], halo_x.at[k, 1], halo_send.at[k, 0], halo_recv.at[k, 0], x_low),
            copy_to(pack.at[k], halo_x.at[k, 0], halo_send.at[k, 1], halo_recv.at[k, 1], x_high),
            copy_to(face_y.at[k, 0], halo_y.at[k, 1], halo_send.at[k, 2], halo_recv.at[k, 2], y_low),
            copy_to(face_y.at[k, 1], halo_y.at[k, 0], halo_send.at[k, 3], halo_recv.at[k, 3], y_high),
            copy_to(field.at[k, 1], field.at[k, NZ + 1], halo_send.at[k, 4], halo_recv.at[k, 4], z_low),
            copy_to(field.at[k, NZ], field.at[k, 0], halo_send.at[k, 5], halo_recv.at[k, 5], z_high),
        ]

    halos = [halo_copies(k) for k in range(SWEEPS + 1)]
    rims = [
        copy_to(rim_pack, rim_x, rim_send.at[0], rim_recv.at[0], x_low),
        copy_to(rim_face, rim_y, rim_send.at[1], rim_recv.at[1], y_low),
        copy_to(bz.at[0], bz.at[NZ], rim_send.at[2], rim_recv.at[2], z_low),
    ]

    def planes(body, carry=None):
        def step(i, carry):
            for j in range(PLANES):
                carry = body(i * PLANES + j, carry)
            return carry

        return lax.fori_loop(0, NZ // PLANES, step, carry)

    def prepare(slots, out):
        def body(z, carry):
            for g in range(GROUPS):
                out[z, g] = lax.select(id0 == theirs[g], slots[0, z, their_part[g]], slots[1, z, their_part[g]])
            return carry

        planes(body, 0)

    def assembled(slots, received, z, g):
        return lax.select(
            id0 == mine[g],
            slots[0, z, my_part[g]],
            lax.select(id1 == mine[g], slots[1, z, my_part[g]], received[z, g]),
        ).astype(F32)

    def packed(k_index, tile_low, tile_high, carry, g):
        spot = k_index * GROUPS + g
        both = jnp.where(lane8 == 0, tile_low, tile_high)
        moved = pltpu.roll(both, 2 * spot + 1, 1)
        return jnp.where(lane8 // 2 == spot, moved, carry)

    loads_f[0].wait()
    prepare(slots_f.at[0], send_f.at[0])
    pl.semaphore_wait(barrier, 6)
    pair_f[0].start()
    for c in (1, 2, 3, 0):
        loads_c[c].wait()
        prepare(slots_c.at[c], send_c.at[c])
        pair_c[c].start()
    loads_f[1].wait()
    prepare(slots_f.at[1], send_f.at[1])
    pair_f[1].start()

    zero_pack = jnp.zeros((ROWS, LANES), F32)

    pair_f[0].wait_recv()

    def start_body(z, carry):
        for g in range(GROUPS):
            value = assembled(slots_f.at[0], recv_f.at[0], z, g)
            field[0, z + 1, g * ROWS : (g + 1) * ROWS, :] = value
            total[z, g * ROWS : (g + 1) * ROWS, :] = value
            if g == 0:
                face_y[0, 0, z] = value[0:1, :]
            if g == GROUPS - 1:
                face_y[0, 1, z] = value[ROWS - 1 : ROWS, :]
            carry = packed(z, value[:, :LANES], value[:, LANES:], carry, g)
        return carry

    pack[0] = planes(start_body, zero_pack)
    for copy in halos[0]:
        copy.start()

    pair_c[1].wait_recv()

    def bx_body(z, carry):
        for g in range(GROUPS):
            value = assembled(slots_c.at[1], recv_c.at[1], z, g)
            bx[z, g * ROWS : (g + 1) * ROWS, :] = value
            carry = packed(z, value[:, :LANES], value[:, LANES:], carry, g)
        return carry

    rim_pack[...] = planes(bx_body, zero_pack)
    rims[0].start()
    pair_c[2].wait_recv()

    def by_body(z, carry):
        for g in range(GROUPS):
            value = assembled(slots_c.at[2], recv_c.at[2], z, g)
            by[z, g * ROWS : (g + 1) * ROWS, :] = value
            if g == 0:
                rim_face[z] = value[0:1, :]
        return carry

    planes(by_body, 0)
    rims[1].start()
    pair_c[3].wait_recv()

    def bz_body(z, carry):
        for g in range(GROUPS):
            bz[z, g * ROWS : (g + 1) * ROWS, :] = assembled(slots_c.at[3], recv_c.at[3], z, g)
        return carry

    planes(bz_body, 0)
    rims[2].start()
    pair_c[0].wait_recv()

    def alpha_body(z, carry):
        for g in range(GROUPS):
            alpha[z, g * ROWS : (g + 1) * ROWS, :] = assembled(slots_c.at[0], recv_c.at[0], z, g)
        return carry

    planes(alpha_body, 0)
    pair_f[1].wait_recv()

    def rhs_body(z, carry):
        for g in range(GROUPS):
            rhs[z, g * ROWS : (g + 1) * ROWS, :] = assembled(slots_f.at[1], recv_f.at[1], z, g)
        return carry

    planes(rhs_body, 0)
    for copy in rims:
        copy.wait_recv()

    def spread(source, z, from_right):
        pieces = []
        for g in range(GROUPS):
            spot = z * GROUPS + g
            shift = 126 - 2 * spot if from_right else lax.rem(LANES - 2 * spot, LANES)
            pieces.append(pltpu.roll(source, shift, 1))
        return jnp.concatenate(pieces, axis=0)

    def shifted_left(low, high, edge):
        low_rolled = pltpu.roll(low, LANES - 1, 1)
        high_rolled = pltpu.roll(high, LANES - 1, 1)
        return jnp.where(last_lane, high_rolled, low_rolled), jnp.where(last_lane, edge, high_rolled)

    def shifted_right(low, high, edge):
        low_rolled = pltpu.roll(low, 1, 1)
        high_rolled = pltpu.roll(high, 1, 1)
        return jnp.where(first_lane, edge, low_rolled), jnp.where(first_lane, low_rolled, high_rolled)

    def up_rows(tile, edge):
        return jnp.where(end_row, jnp.broadcast_to(edge, (NY, LANES)), pltpu.roll(tile, NY - 1, 0))

    def down_rows(tile, edge):
        return jnp.where(top_row, jnp.broadcast_to(edge, (NY, LANES)), pltpu.roll(tile, 1, 0))

    halves = (slice(0, LANES), slice(LANES, NX))

    rim_values = rim_x[...]

    def scale_body(z, carry):
        upper_x = shifted_left(bx[z, :, :LANES], bx[z, :, LANES:], spread(rim_values, z, True))
        for j, part in enumerate(halves):
            faces = [bx[z, :, part], upper_x[j], by[z, :, part]]
            faces.append(up_rows(faces[2], rim_y[z, :, part]))
            faces.append(bz[z, :, part])
            faces.append(bz[z + 1, :, part])
            centre = alpha[z, :, part]
            for face in faces:
                centre = centre + face
            inverse = 1.0 / centre
            diag[z, :, part] = centre
            for i, face in enumerate(faces):
                near[i, z, :, part] = inverse * face
            scaled[z, :, part] = inverse * rhs[z, :, part]
        return carry

    planes(scale_body, 0)

    def apply(k):
        for copy in halos[k]:
            copy.wait_recv()
        from_low = halo_x[k, 0]
        from_high = halo_x[k, 1]
        last = k == SWEEPS

        def body(z, carry):
            low, high = field[k, z + 1, :, :LANES], field[k, z + 1, :, LANES:]
            x_before = shifted_right(low, high, spread(from_low, z, False))
            x_after = shifted_left(low, high, spread(from_high, z, True))
            fresh = []
            for j, part in enumerate(halves):
                here = (low, high)[j]
                value = scaled[z, :, part] - here
                value = value + near[0, z, :, part] * x_before[j] + near[1, z, :, part] * x_after[j]
                value = value + near[2, z, :, part] * down_rows(here, halo_y[k, 0, z, :, part])
                value = value + near[3, z, :, part] * up_rows(here, halo_y[k, 1, z, :, part])
                value = value + near[4, z, :, part] * field[k, z, :, part]
                value = value + near[5, z, :, part] * field[k, z + 2, :, part]
                if last:
                    resid[z, :, part] = diag[z, :, part] * value
                    continue
                scaled[z, :, part] = value
                step = SECOND[k] * value
                if k > 0:
                    step = step + FIRST[k] * here
                field[k + 1, z + 1, :, part] = step
                total[z, :, part] = total[z, :, part] + step
                face_y[k + 1, 0, z, :, part] = step[0:1, :]
                face_y[k + 1, 1, z, :, part] = step[NY - 1 : NY, :]
                fresh.append(step)
            if last:
                return carry
            for g in range(GROUPS):
                rows = slice(g * ROWS, (g + 1) * ROWS)
                carry = packed(z, fresh[0][rows], fresh[1][rows], carry, g)
            return carry

        return planes(body, zero_pack)

    for k in range(SWEEPS):
        pack[k + 1] = apply(k)
        for copy in halos[k + 1]:
            copy.start()
    x_out = pltpu.make_async_copy(total, x_hbm, out_sem.at[0])
    x_out.start()
    apply(SWEEPS)
    r_out = pltpu.make_async_copy(resid, r_hbm, out_sem.at[1])
    r_out.start()
    for copy in pair_f + pair_c + rims:
        copy.wait_send()
    for copies in halos:
        for copy in copies:
            copy.wait_send()
    x_out.wait()
    r_out.wait()


def local(old_fields, old_coef, held_slabs):
    slots = old_fields.shape[1]
    fields = old_fields.reshape(2, slots, NZ, 2, ROWS, NX)
    coef = old_coef.reshape(4, slots, NZ, 2, ROWS, NX)
    brick = (NZ, NY, NX)
    rounds = SWEEPS + 1
    dma = pltpu.SemaphoreType.DMA
    anywhere = pl.BlockSpec(memory_space=pl.ANY)
    return pl.pallas_call(
        kernel,
        out_shape=(jax.ShapeDtypeStruct(brick, F32), jax.ShapeDtypeStruct(brick, F32)),
        in_specs=[anywhere, anywhere, pl.BlockSpec(memory_space=pltpu.SMEM)],
        out_specs=(anywhere, anywhere),
        scratch_shapes=[
            pltpu.VMEM((2, slots, NZ, 2, ROWS, NX), F32),
            pltpu.VMEM((4, slots, NZ, 2, ROWS, NX), BF16),
            pltpu.VMEM((2, NZ, GROUPS, ROWS, NX), F32),
            pltpu.VMEM((4, NZ, GROUPS, ROWS, NX), BF16),
            pltpu.VMEM((2, NZ, GROUPS, ROWS, NX), F32),
            pltpu.VMEM((4, NZ, GROUPS, ROWS, NX), BF16),
            pltpu.VMEM((rounds, NZ + 2, NY, NX), F32),
            pltpu.VMEM(brick, F32),
            pltpu.VMEM(brick, F32),
            pltpu.VMEM(brick, F32),
            pltpu.VMEM((NZ + 1, NY, NX), F32),
            pltpu.VMEM(brick, F32),
            pltpu.VMEM((6, NZ, NY, NX), F32),
            pltpu.VMEM(brick, F32),
            pltpu.VMEM(brick, F32),
            pltpu.VMEM(brick, F32),
            pltpu.VMEM(brick, F32),
            pltpu.VMEM((rounds, ROWS, LANES), F32),
            pltpu.VMEM((rounds, 2, NZ, 1, NX), F32),
            pltpu.VMEM((rounds, 2, ROWS, LANES), F32),
            pltpu.VMEM((rounds, 2, NZ, 1, NX), F32),
            pltpu.VMEM((ROWS, LANES), F32),
            pltpu.VMEM((NZ, 1, NX), F32),
            pltpu.VMEM((ROWS, LANES), F32),
            pltpu.VMEM((NZ, 1, NX), F32),
            dma((6,)),
            dma((6,)),
            dma((6,)),
            dma((rounds, 6)),
            dma((rounds, 6)),
            dma((3,)),
            dma((3,)),
            dma((2,)),
        ],
        compiler_params=pltpu.CompilerParams(
            collective_id=0, has_side_effects=True, vmem_limit_bytes=48 << 20
        ),
        name="smooth",
    )(fields, coef, held_slabs)


def solution(mesh):
    in_specs = (
        P(None, "gy", "gz", None, "gx"),
        P(None, "gy", "gz", None, "gx"),
        P("gy", "gz", "gx"),
    )
    out_specs = (P("gz", "gy", "gx"), P("gz", "gy", "gx"))
    return jax.shard_map(local, mesh=mesh, in_specs=in_specs, out_specs=out_specs, check_vma=False)
```

time: 149 us -> 39.7 us (0.27)
  the two profiles are of different devices: /device:TPU:24 before, /device:TPU:1 now
where the time goes in v1:
time: 39.7 us; the launch traced here: 39.5 us
  Pallas kernels  34.1 us (86%)
  local copies, waits for them, and re-layouts  4.68 us (12%)
  between operations  0.65 us (2%)
    pallas_call x1, Pallas kernels, local(): pl.pallas_call(kernel, out_shape=(jax.ShapeDtypeStruct(brick, F32), jax.S...  34.1 us
    unnamed x9, local copies, waits for them, and re-layouts  4.68 us

profile of v1, /device:TPU:1, one launch (start us, length us, event | category | flops | bytes accessed | tf_op | source)
XLA Modules:
  0.0 39.5 jit_solution(16362715077557923704)
XLA Ops:
  0.6 0.0 copy-start.2
  0.6 0.6 %copy-done.2 = s32[2,1,1]{0,2,1:T(1,128)S(1)} copy-done((s32[2,1,1]{0,2,1:T(1,128)S(1)}, s32[2,1,1]{0,2,1:T(1,128)}, u32[]{:S(2)}) %copy-start.2) | copy-done | bytes 32
  1.3 0.1 copy.5.held_ref
  1.4 0.0 copy-start
  1.4 1.2 %copy-done = f32[2,2,16,16,256]{4,3,2,1,0:T(8,128)S(1)} copy-done((f32[2,2,16,16,256]{4,3,2,1,0:T(8,128)S(1)}, f32[2,2,16,16,256]{4,3,2,1,0:T(8,128)}, u32[]{:S(2)}) %copy-start) | copy-done | bytes 1048600
  2.6 0.0 copy-start.1
  2.6 1.2 %copy-done.1 = bf16[4,2,16,16,256]{4,3,2,1,0:T(8,128)(2,1)S(1)} copy-done((bf16[4,2,16,16,256]{4,3,2,1,0:T(8,128)(2,1)S(1)}, bf16[4,2,16,16,256]{4,3,2,1,0:T(8,128)(2,1)}, u32[]{:S(2)}) %copy-start.1) | copy-done | bytes 1048600
  3.8 34.1 %smooth.1 = (f32[16,24,256]{2,1,0:T(8,128)S(1)}, f32[16,24,256]{2,1,0:T(8,128)S(1)}) custom-call(f32[2,2,16,2,8,256]{5,4,3,2,1,0:T(8,128)S(1)} %bitcast.2, bf16[4,2,16,2,8,256]{5,4,3,2,1,0:T(8,128)(2,1)S(1)} %bitcast.3, s32[2,1,1]{2,1,0:T(1,128)S(1)} %copy.5.held_ref), custom_call_target="tpu_custom_call" | custom-call | tf_op jit(solution)/shard_map/smooth/pallas_call | solution.py:345
  38.0 0.7 %copy.8 = f32[16,24,256]{2,1,0:T(8,128)} copy(f32[16,24,256]{2,1,0:T(8,128)S(1)} %get-tuple-element.4) | data formatting | bytes 786432
  38.7 0.7 %copy.9 = f32[16,24,256]{2,1,0:T(8,128)} copy(f32[16,24,256]{2,1,0:T(8,128)S(1)} %get-tuple-element.5) | data formatting | bytes 786432
Async XLA Ops:
  0.6 0.7 %copy-start.2 = (s32[2,1,1]{0,2,1:T(1,128)S(1)}, s32[2,1,1]{0,2,1:T(1,128)}, u32[]{:S(2)}) copy-start(s32[2,1,1]{0,2,1:T(1,128)} %param.5) | copy-start | bytes 28
  1.4 1.2 %copy-start = (f32[2,2,16,16,256]{4,3,2,1,0:T(8,128)S(1)}, f32[2,2,16,16,256]{4,3,2,1,0:T(8,128)}, u32[]{:S(2)}) copy-start(f32[2,2,16,16,256]{4,3,2,1,0:T(8,128)} %param.3) | copy-start | bytes 3145732
  2.6 1.2 %copy-start.1 = (bf16[4,2,16,16,256]{4,3,2,1,0:T(8,128)(2,1)S(1)}, bf16[4,2,16,16,256]{4,3,2,1,0:T(8,128)(2,1)}, u32[]{:S(2)}) copy-start(bf16[4,2,16,16,256]{4,3,2,1,0:T(8,128)(2,1)} %param.4) | copy-start | bytes 3145732

commit v2 on v1

v2 whole, which is shorter than its diff:
```python
import functools
import jax
import jax.numpy as jnp
from jax import lax
from jax.experimental import pallas as pl
from jax.experimental.pallas import tpu as pltpu
from jax.sharding import PartitionSpec as P

SWEEPS = 4
NZ = 16
NY = 24
NX = 256
ROWS = 8
LANES = 128
GROUPS = NY // ROWS
MESH = pl.DeviceIdType.MESH
F32 = jnp.float32
BF16 = jnp.bfloat16


def chebyshev_weights(count):
    low_bound = 0.25
    high_bound = 2.0
    centre_value = 0.5 * (high_bound + low_bound)
    half_width = 0.5 * (high_bound - low_bound)
    ratio_value = centre_value / half_width
    damping = 1.0 / ratio_value
    first_list = [0.0]
    second_list = [1.0 / centre_value]
    for step_index in range(1, count):
        damping_next = 1.0 / (2.0 * ratio_value - damping)
        first_list.append(damping_next * damping)
        second_list.append(2.0 * damping_next / half_width)
        damping = damping_next
    return first_list, second_list


FIRST, SECOND = chebyshev_weights(SWEEPS)


def ring(axis):
    count = lax.axis_size(axis)
    me = lax.axis_index(axis)
    low = {axis: lax.rem(me + count - 1, count)}
    high = {axis: lax.rem(me + 1, count)}
    return low, high


def kernel(
    fields_hbm, coef_hbm, held_hbm, x_hbm, r_hbm,
    slots_f, slots_c, send_f, send_c, recv_f, recv_c,
    field, alpha, bx, by, bz, rhs, near, edge_y, edge_x, diag, scaled, total, resid,
    pack, face_y, halo_x, halo_y, rim_pack, rim_face, rim_x, rim_y, held_ref,
    load_sem, held_sem, pair_send, pair_recv, halo_send, halo_recv, rim_send, rim_recv, out_sem,
):
    group = lax.axis_index("gy")
    half = lax.rem(group, 2)
    first_slab = 3 * (group // 2)
    partner = {"gy": group + 1 - 2 * half}
    x_low, x_high = ring("gx")
    y_low, y_high = ring("gy")
    z_low, z_high = ring("gz")

    barrier = pltpu.get_barrier_semaphore()
    for neighbour in (x_low, x_high, y_low, y_high, z_low, z_high):
        pl.semaphore_signal(barrier, inc=1, device_id=neighbour, device_id_type=MESH)

    load_held = pltpu.make_async_copy(held_hbm, held_ref, held_sem.at[0])
    loads_f = [pltpu.make_async_copy(fields_hbm.at[c], slots_f.at[c], load_sem.at[c]) for c in range(2)]
    loads_c = [pltpu.make_async_copy(coef_hbm.at[c], slots_c.at[c], load_sem.at[2 + c]) for c in range(4)]
    load_held.start()
    loads_f[0].start()
    for c in (1, 2, 3, 0):
        loads_c[c].start()
    loads_f[1].start()
    load_held.wait()

    id0 = held_ref[0, 0, 0]
    id1 = held_ref[0, 0, 1]
    mine = [first_slab + (3 * half + g) // 2 for g in range(GROUPS)]
    theirs = [first_slab + (3 * (1 - half) + g) // 2 for g in range(GROUPS)]
    my_part = [lax.rem(half + g, 2) for g in range(GROUPS)]
    their_part = [lax.rem(1 - half + g, 2) for g in range(GROUPS)]

    row8 = lax.broadcasted_iota(jnp.int32, (ROWS, LANES), 0)
    row = lax.broadcasted_iota(jnp.int32, (NY, LANES), 0)
    lane = lax.broadcasted_iota(jnp.int32, (NY, LANES), 1)
    lane8 = lax.broadcasted_iota(jnp.int32, (ROWS, LANES), 1)
    end_row = row == NY - 1
    first_lane = lane == 0
    last_lane = lane == LANES - 1
    spots = lane8 // 2

    def copy_to(source, target, send_sem, recv_sem, device):
        return pltpu.make_async_remote_copy(
            src_ref=source, dst_ref=target, send_sem=send_sem, recv_sem=recv_sem,
            device_id=device, device_id_type=MESH,
        )

    pair_f = [copy_to(send_f.at[c], recv_f.at[c], pair_send.at[c], pair_recv.at[c], partner) for c in range(2)]
    pair_c = [
        copy_to(send_c.at[c], recv_c.at[c], pair_send.at[2 + c], pair_recv.at[2 + c], partner) for c in range(4)
    ]

    def halo_copies(k):
        return [
            copy_to(field.at[k, 1], field.at[k, NZ + 1], halo_send.at[k, 4], halo_recv.at[k, 4], z_low),
            copy_to(field.at[k, NZ], field.at[k, 0], halo_send.at[k, 5], halo_recv.at[k, 5], z_high),
            copy_to(face_y.at[k, 0], halo_y.at[k, 1], halo_send.at[k, 2], halo_recv.at[k, 2], y_low),
            copy_to(face_y.at[k, 1], halo_y.at[k, 0], halo_send.at[k, 3], halo_recv.at[k, 3], y_high),
            copy_to(pack.at[k], halo_x.at[k, 1], halo_send.at[k, 0], halo_recv.at[k, 0], x_low),
            copy_to(pack.at[k], halo_x.at[k, 0], halo_send.at[k, 1], halo_recv.at[k, 1], x_high),
        ]

    halos = [halo_copies(k) for k in range(SWEEPS + 1)]
    rims = [
        copy_to(rim_pack, rim_x, rim_send.at[0], rim_recv.at[0], x_low),
        copy_to(rim_face, rim_y, rim_send.at[1], rim_recv.at[1], y_low),
        copy_to(bz.at[0], bz.at[NZ], rim_send.at[2], rim_recv.at[2], z_low),
    ]

    def planes(body, carry=0, first=0, last=NZ):
        return lax.fori_loop(first, last, body, carry, unroll=True)

    def prepare(slots, out):
        def body(z, carry):
            for g in range(GROUPS):
                out[z, g] = lax.select(id0 == theirs[g], slots[0, z, their_part[g]], slots[1, z, their_part[g]])
            return carry

        planes(body)

    def assembled(slots, received, z, g):
        return lax.select(
            id0 == mine[g],
            slots[0, z, my_part[g]],
            lax.select(id1 == mine[g], slots[1, z, my_part[g]], received[z, g]),
        ).astype(F32)

    def packed(z, g, tile_low, tile_high, carry):
        spot = z * GROUPS + g
        both = jnp.where(lane8 == 0, tile_low, tile_high)
        moved = pltpu.roll(both, 2 * spot + 1, 1)
        return jnp.where(spots == spot, moved, carry)

    loads_f[0].wait()
    prepare(slots_f.at[0], send_f.at[0])
    pl.semaphore_wait(barrier, 6)
    pair_f[0].start()
    for c in (1, 2, 3, 0):
        loads_c[c].wait()
        prepare(slots_c.at[c], send_c.at[c])
        pair_c[c].start()
    loads_f[1].wait()
    prepare(slots_f.at[1], send_f.at[1])
    pair_f[1].start()

    zero_pack = jnp.zeros((ROWS, LANES), F32)

    pair_f[0].wait_recv()

    def start_body(z, carry):
        for g in range(GROUPS):
            value = assembled(slots_f.at[0], recv_f.at[0], z, g)
            field[0, z + 1, g * ROWS : (g + 1) * ROWS, :] = value
            total[z, g * ROWS : (g + 1) * ROWS, :] = value
            if g == 0:
                face_y[0, 0, z] = value[0:1, :]
            if g == GROUPS - 1:
                face_y[0, 1, z] = value[ROWS - 1 : ROWS, :]
            carry = packed(z, g, value[:, :LANES], value[:, LANES:], carry)
        return carry

    pack[0] = planes(start_body, zero_pack)
    for copy in halos[0]:
        copy.start()

    pair_c[1].wait_recv()

    def bx_body(z, carry):
        for g in range(GROUPS):
            value = assembled(slots_c.at[1], recv_c.at[1], z, g)
            bx[z, g * ROWS : (g + 1) * ROWS, :] = value
            carry = packed(z, g, value[:, :LANES], value[:, LANES:], carry)
        return carry

    rim_pack[...] = planes(bx_body, zero_pack)
    rims[0].start()
    pair_c[2].wait_recv()

    def by_body(z, carry):
        for g in range(GROUPS):
            value = assembled(slots_c.at[2], recv_c.at[2], z, g)
            by[z, g * ROWS : (g + 1) * ROWS, :] = value
            if g == 0:
                rim_face[z] = value[0:1, :]
        return carry

    planes(by_body)
    rims[1].start()

    def plain(slots, received, out):
        def body(z, carry):
            for g in range(GROUPS):
                out[z, g * ROWS : (g + 1) * ROWS, :] = assembled(slots, received, z, g)
            return carry

        planes(body)

    pair_c[3].wait_recv()
    plain(slots_c.at[3], recv_c.at[3], bz)
    rims[2].start()
    pair_c[0].wait_recv()
    plain(slots_c.at[0], recv_c.at[0], alpha)
    pair_f[1].wait_recv()
    plain(slots_f.at[1], recv_f.at[1], rhs)
    for copy in rims:
        copy.wait_recv()

    halves = (slice(0, LANES), slice(LANES, NX))
    group_rows = [slice(g * ROWS, (g + 1) * ROWS) for g in range(GROUPS)]
    rim_values = rim_x[...]

    def scale_body(z, carry):
        low_rolled = pltpu.roll(bx[z, :, :LANES], LANES - 1, 1)
        high_rolled = pltpu.roll(bx[z, :, LANES:], LANES - 1, 1)
        edge = jnp.concatenate(
            [pltpu.roll(rim_values, 126 - 2 * (z * GROUPS + g), 1) for g in range(GROUPS)], axis=0
        )
        upper_x = (jnp.where(last_lane, high_rolled, low_rolled), jnp.where(last_lane, edge, high_rolled))
        before = []
        after = []
        for j, part in enumerate(halves):
            here_y = by[z, :, part]
            upper_y = jnp.where(
                end_row, jnp.broadcast_to(rim_y[z, :, part], (NY, LANES)), pltpu.roll(here_y, NY - 1, 0)
            )
            faces = [bx[z, :, part], upper_x[j], here_y, upper_y, bz[z, :, part], bz[z + 1, :, part]]
            centre = alpha[z, :, part]
            for face in faces:
                centre = centre + face
            inverse = 1.0 / centre
            diag[z, :, part] = centre
            scaled[z, :, part] = inverse * rhs[z, :, part]
            weights = [inverse * face for face in faces]
            before.append(weights[0])
            after.append(weights[1])
            if j == 0:
                weights[0] = jnp.where(first_lane, 0.0, weights[0])
            else:
                weights[1] = jnp.where(last_lane, 0.0, weights[1])
            edge_y[0, z, :, part] = jnp.where(row8 == 0, weights[2][:ROWS], 0.0)
            edge_y[1, z, :, part] = jnp.where(row8 == ROWS - 1, weights[3][NY - ROWS :], 0.0)
            weights[2] = jnp.where(row == 0, 0.0, weights[2])
            weights[3] = jnp.where(end_row, 0.0, weights[3])
            for i, weight in enumerate(weights):
                near[i, z, :, part] = weight
        for g, rows in enumerate(group_rows):
            carry = packed(z, g, before[0][rows], after[1][rows], carry)
        return carry

    edge_x[...] = planes(scale_body, zero_pack)

    def inner(k, z, first, last):
        low, high = field[k, z + 1, :, :LANES], field[k, z + 1, :, LANES:]
        low_after, high_after = pltpu.roll(low, LANES - 1, 1), pltpu.roll(high, LANES - 1, 1)
        low_before, high_before = pltpu.roll(low, 1, 1), pltpu.roll(high, 1, 1)
        x_before = (low_before, jnp.where(first_lane, low_before, high_before))
        x_after = (jnp.where(last_lane, high_after, low_after), high_after)
        for j, part in enumerate(halves):
            here = (low, high)[j]
            value = scaled[z, :, part] - here
            value = value + near[0, z, :, part] * x_before[j] + near[1, z, :, part] * x_after[j]
            value = value + near[2, z, :, part] * pltpu.roll(here, 1, 0)
            value = value + near[3, z, :, part] * pltpu.roll(here, NY - 1, 0)
            if not first:
                value = value + near[4, z, :, part] * field[k, z, :, part]
            if not last:
                value = value + near[5, z, :, part] * field[k, z + 2, :, part]
            scaled[z, :, part] = value

    def outer(k, z, first, last, sides, carry):
        fresh = [[], []]
        for g, rows in enumerate(group_rows):
            moved = pltpu.roll(sides, LANES - 1 - 2 * (z * GROUPS + g), 1)
            for j, part in enumerate(halves):
                value = scaled[z, rows, part] + jnp.where(lane8 == (0, LANES - 1)[j], moved, 0.0)
                if g == 0:
                    value = value + edge_y[0, z, :, part] * jnp.broadcast_to(halo_y[k, 0, z, :, part], (ROWS, LANES))
                if g == GROUPS - 1:
                    value = value + edge_y[1, z, :, part] * jnp.broadcast_to(halo_y[k, 1, z, :, part], (ROWS, LANES))
                if first:
                    value = value + near[4, z, rows, part] * field[k, z, rows, part]
                if last:
                    value = value + near[5, z, rows, part] * field[k, z + 2, rows, part]
                if k == SWEEPS:
                    resid[z, rows, part] = diag[z, rows, part] * value
                    continue
                scaled[z, rows, part] = value
                step = SECOND[k] * value
                if k > 0:
                    step = step + FIRST[k] * field[k, z + 1, rows, part]
                field[k + 1, z + 1, rows, part] = step
                total[z, rows, part] = total[z, rows, part] + step
                if g == 0:
                    face_y[k + 1, 0, z, :, part] = step[0:1, :]
                if g == GROUPS - 1:
                    face_y[k + 1, 1, z, :, part] = step[ROWS - 1 : ROWS, :]
                fresh[j].append(step)
            if k < SWEEPS:
                carry = packed(z, g, fresh[0][g], fresh[1][g], carry)
        return carry

    def apply(k):
        inner(k, 0, True, False)

        def inner_body(z, carry):
            inner(k, z, False, False)
            return carry

        planes(inner_body, 0, 1, NZ - 1)
        inner(k, NZ - 1, False, True)
        for copy in halos[k]:
            copy.wait_recv()
        from_low = pltpu.roll(halo_x[k, 0], 1, 1)
        from_high = pltpu.roll(halo_x[k, 1], LANES - 1, 1)
        sides = edge_x[...] * jnp.where(lane8 - 2 * spots == 1, from_low, from_high)
        carry = outer(k, 0, True, False, sides, zero_pack)
        carry = planes(lambda z, carry: outer(k, z, False, False, sides, carry), carry, 1, NZ - 1)
        return outer(k, NZ - 1, False, True, sides, carry)

    for k in range(SWEEPS):
        pack[k + 1] = apply(k)
        for copy in halos[k + 1]:
            copy.start()
    x_out = pltpu.make_async_copy(total, x_hbm, out_sem.at[0])
    x_out.start()
    apply(SWEEPS)
    r_out = pltpu.make_async_copy(resid, r_hbm, out_sem.at[1])
    r_out.start()
    for copy in pair_f + pair_c + rims:
        copy.wait_send()
    for copies in halos:
        for copy in copies:
            copy.wait_send()
    x_out.wait()
    r_out.wait()


def emit(x_ref, r_ref, x_out, r_out, sem):
    first = pltpu.make_async_copy(x_ref, x_out, sem.at[0])
    second = pltpu.make_async_copy(r_ref, r_out, sem.at[1])
    first.start()
    second.start()
    first.wait()
    second.wait()


def local(old_fields, old_coef, held_slabs):
    slots = old_fields.shape[1]
    fields = old_fields.reshape(2, slots, NZ, 2, ROWS, NX)
    coef = old_coef.reshape(4, slots, NZ, 2, ROWS, NX)
    brick = (NZ, NY, NX)
    rounds = SWEEPS + 1
    dma = pltpu.SemaphoreType.DMA
    anywhere = pl.BlockSpec(memory_space=pl.ANY)
    hbm = pl.BlockSpec(memory_space=pltpu.HBM)
    held = jnp.transpose(held_slabs, (1, 2, 0))
    results = pl.pallas_call(
        kernel,
        out_shape=(jax.ShapeDtypeStruct(brick, F32), jax.ShapeDtypeStruct(brick, F32)),
        in_specs=[hbm, hbm, hbm],
        out_specs=(anywhere, anywhere),
        scratch_shapes=[
            pltpu.VMEM((2, slots, NZ, 2, ROWS, NX), F32),
            pltpu.VMEM((4, slots, NZ, 2, ROWS, NX), BF16),
            pltpu.VMEM((2, NZ, GROUPS, ROWS, NX), F32),
            pltpu.VMEM((4, NZ, GROUPS, ROWS, NX), BF16),
            pltpu.VMEM((2, NZ, GROUPS, ROWS, NX), F32),
            pltpu.VMEM((4, NZ, GROUPS, ROWS, NX), BF16),
            pltpu.VMEM((rounds, NZ + 2, NY, NX), F32),
            pltpu.VMEM(brick, F32),
            pltpu.VMEM(brick, F32),
            pltpu.VMEM(brick, F32),
            pltpu.VMEM((NZ + 1, NY, NX), F32),
            pltpu.VMEM(brick, F32),
            pltpu.VMEM((6, NZ, NY, NX), F32),
            pltpu.VMEM((2, NZ, ROWS, NX), F32),
            pltpu.VMEM((ROWS, LANES), F32),
            pltpu.VMEM(brick, F32),
            pltpu.VMEM(brick, F32),
            pltpu.VMEM(brick, F32),
            pltpu.VMEM(brick, F32),
            pltpu.VMEM((rounds, ROWS, LANES), F32),
            pltpu.VMEM((rounds, 2, NZ, 1, NX), F32),
            pltpu.VMEM((rounds, 2, ROWS, LANES), F32),
            pltpu.VMEM((rounds, 2, NZ, 1, NX), F32),
            pltpu.VMEM((ROWS, LANES), F32),
            pltpu.VMEM((NZ, 1, NX), F32),
            pltpu.VMEM((ROWS, LANES), F32),
            pltpu.VMEM((NZ, 1, NX), F32),
            pltpu.SMEM((1, 1, slots), jnp.int32),
            dma((6,)),
            dma((1,)),
            dma((6,)),
            dma((6,)),
            dma((rounds, 6)),
            dma((rounds, 6)),
            dma((3,)),
            dma((3,)),
            dma((2,)),
        ],
        compiler_params=pltpu.CompilerParams(
            collective_id=0, has_side_effects=True, vmem_limit_bytes=55767040
        ),
        name="smooth",
    )(fields, coef, held)
    return pl.pallas_call(
        emit,
        out_shape=(jax.ShapeDtypeStruct(brick, F32), jax.ShapeDtypeStruct(brick, F32)),
        in_specs=[anywhere, anywhere],
        out_specs=(hbm, hbm),
        scratch_shapes=[dma((2,))],
        compiler_params=pltpu.CompilerParams(vmem_limit_bytes=1 << 20),
        name="emit",
    )(*results)


def solution(mesh):
    in_specs = (
        P(None, "gy", "gz", None, "gx"),
        P(None, "gy", "gz", None, "gx"),
        P("gy", "gz", "gx"),
    )
    out_specs = (P("gz", "gy", "gx"), P("gz", "gy", "gx"))
    return jax.shard_map(local, mesh=mesh, in_specs=in_specs, out_specs=out_specs, check_vma=False)
```

time: 39.7 us -> 33.7 us (0.85)
  local copies, waits for them, and re-layouts: 4.68 us -> 0.65 us
  Pallas kernels: 34.1 us -> 31.8 us
    unnamed x9 -> x2, local copies, waits for them, and re-layouts: 4.68 us -> 0.65 us
    pallas_call x1, Pallas kernels: 34.1 us -> 30.9 us  [local(): pl.pallas_call(kernel, out_shape=(jax.ShapeDtypeStruct(brick, F32), jax.S...]
    pallas_call x0 -> x1, Pallas kernels: none -> 0.89 us  [local(): pl.pallas_call(emit, out_shape=(jax.ShapeDtypeStruct(brick, F32), jax.Sha...]
where the time goes in v2:
time: 33.7 us; the launch traced here: 33.1 us
  Pallas kernels  31.8 us (94%)
  local copies, waits for them, and re-layouts  0.65 us (2%)
  between operations  0.65 us (2%)
    pallas_call x1, Pallas kernels, local(): pl.pallas_call(kernel, out_shape=(jax.ShapeDtypeStruct(brick, F32), jax.S...  30.9 us
    pallas_call x1, Pallas kernels, local(): pl.pallas_call(emit, out_shape=(jax.ShapeDtypeStruct(brick, F32), jax.Sha...  0.89 us

profile of v2, /device:TPU:1, one launch (start us, length us, event | category | flops | bytes accessed | tf_op | source)
XLA Modules:
  0.0 33.1 jit_solution(10139504650679535945)
XLA Ops:
  0.6 0.0 copy-start
  0.6 0.6 %copy-done = s32[2,1,1]{0,2,1:T(1,128)S(1)} copy-done((s32[2,1,1]{0,2,1:T(1,128)S(1)}, s32[2,1,1]{0,2,1:T(1,128)}, u32[]{:S(2)}) %copy-start) | copy-done | bytes 32
  1.3 30.9 %smooth.1 = (f32[16,24,256]{2,1,0:T(8,128)S(1)}, f32[16,24,256]{2,1,0:T(8,128)S(1)}) custom-call(f32[2,2,16,2,8,256]{5,4,3,2,1,0:T(8,128)} %bitcast.4, bf16[4,2,16,2,8,256]{5,4,3,2,1,0:T(8,128)(2,1)} %bitcast.5, s32[1,1,2]{2,1,0:T(1,128)S(1)} %bitcast.3), custom_call_target="tpu_custom_call" | custom-call | tf_op jit(solution)/shard_map/smooth/pallas_call | solution.py:369
  32.2 0.9 %emit.1 = (f32[16,24,256]{2,1,0:T(8,128)}, f32[16,24,256]{2,1,0:T(8,128)}) custom-call(f32[16,24,256]{2,1,0:T(8,128)S(1)} %get-tuple-element.4.x_ref, f32[16,24,256]{2,1,0:T(8,128)S(1)} %get-tuple-element.5.r_ref), custom_call_target="tpu_custom_call" | custom-call | tf_op jit(solution)/shard_map/emit/pallas_call | solution.py:418
Async XLA Ops:
  0.6 0.7 %copy-start = (s32[2,1,1]{0,2,1:T(1,128)S(1)}, s32[2,1,1]{0,2,1:T(1,128)}, u32[]{:S(2)}) copy-start(s32[2,1,1]{0,2,1:T(1,128)} %param.5) | copy-start | bytes 28

commit v3 on v2

--- a/solution.py
+++ b/solution.py
@@ -49,9 +49,11 @@
 def kernel(
     fields_hbm, coef_hbm, held_hbm, x_hbm, r_hbm,
     slots_f, slots_c, send_f, send_c, recv_f, recv_c,
-    field, alpha, bx, by, bz, rhs, near, edge_y, edge_x, diag, scaled, total, resid,
-    pack, face_y, halo_x, halo_y, rim_pack, rim_face, rim_x, rim_y, held_ref,
+    field, alpha, bx, by, bz, rhs, near, edge_y, edge_x, diag, inverse_ref, scaled, total, resid,
+    pack, face_y, halo_x, halo_y, rim_pack, rim_face, rim_x, rim_y, beta_pack,
+    sent_z, got_z, sent_y, got_y, sent_x, got_x, sent_yz, got_yz, sent_q, got_xz, got_xy, held_ref,
     load_sem, held_sem, pair_send, pair_recv, halo_send, halo_recv, rim_send, rim_recv, out_sem,
+    both_send, both_recv,
 ):
     group = lax.axis_index("gy")
     half = lax.rem(group, 2)
@@ -62,7 +64,12 @@
     z_low, z_high = ring("gz")
 
     barrier = pltpu.get_barrier_semaphore()
-    for neighbour in (x_low, x_high, y_low, y_high, z_low, z_high):
+    x_sides, y_sides, z_sides = (x_low, x_high), (y_low, y_high), (z_low, z_high)
+    faces = [x_low, x_high, y_low, y_high, z_low, z_high]
+    edges = [{**a, **b} for a in z_sides for b in y_sides]
+    edges += [{**a, **b} for a in x_sides for b in z_sides]
+    edges += [{**a, **b} for a in x_sides for b in y_sides]
+    for neighbour in faces + edges:
         pl.semaphore_signal(barrier, inc=1, device_id=neighbour, device_id_type=MESH)
 
     load_held = pltpu.make_async_copy(held_hbm, held_ref, held_sem.at[0])
@@ -112,7 +119,35 @@
             copy_to(pack.at[k], halo_x.at[k, 0], halo_send.at[k, 1], halo_recv.at[k, 1], x_high),
         ]
 
-    halos = [halo_copies(k) for k in range(SWEEPS + 1)]
+    first_halos = halo_copies(0)
+
+    def edge_copies(r):
+        copies = []
+        for a in range(2):
+            for b in range(2):
+                copies.append((sent_q.at[r], got_xy.at[r, 1 - a, 1 - b], {**x_sides[a], **y_sides[b]}))
+        for a in range(2):
+            for b in range(2):
+                copies.append((sent_q.at[r], got_xz.at[r, 1 - a, 1 - b], {**x_sides[a], **z_sides[b]}))
+        for a in range(2):
+            for b in range(2):
+                copies.append((sent_yz.at[r, a, b], got_yz.at[r, 1 - a, 1 - b], {**z_sides[a], **y_sides[b]}))
+        return [copy_to(m[0], m[1], both_send.at[r, i], both_recv.at[r, i], m[2]) for i, m in enumerate(copies)]
+
+    def face_copies(r):
+        count = 3 - r
+        copies = [
+            (sent_x.at[r, pl.ds(0, count)], got_x.at[r, 1 - a, pl.ds(0, count)], x_sides[a]) for a in range(2)
+        ]
+        copies += [
+            (sent_y.at[r, a, pl.ds(0, count)], got_y.at[r, 1 - a, pl.ds(0, count)], y_sides[a]) for a in range(2)
+        ]
+        copies += [
+            (sent_z.at[r, a, pl.ds(0, count)], got_z.at[r, 1 - a, pl.ds(0, count)], z_sides[a]) for a in range(2)
+        ]
+        return [
+            copy_to(m[0], m[1], both_send.at[r, 12 + i], both_recv.at[r, 12 + i], m[2]) for i, m in enumerate(copies)
+        ]
     rims = [
         copy_to(rim_pack, rim_x, rim_send.at[0], rim_recv.at[0], x_low),
         copy_to(rim_face, rim_y, rim_send.at[1], rim_recv.at[1], y_low),
@@ -145,7 +180,7 @@
 
     loads_f[0].wait()
     prepare(slots_f.at[0], send_f.at[0])
-    pl.semaphore_wait(barrier, 6)
+    pl.semaphore_wait(barrier, len(faces) + len(edges))
     pair_f[0].start()
     for c in (1, 2, 3, 0):
         loads_c[c].wait()
@@ -163,7 +198,6 @@
         for g in range(GROUPS):
             value = assembled(slots_f.at[0], recv_f.at[0], z, g)
             field[0, z + 1, g * ROWS : (g + 1) * ROWS, :] = value
-            total[z, g * ROWS : (g + 1) * ROWS, :] = value
             if g == 0:
                 face_y[0, 0, z] = value[0:1, :]
             if g == GROUPS - 1:
@@ -172,7 +206,7 @@
         return carry
 
     pack[0] = planes(start_body, zero_pack)
-    for copy in halos[0]:
+    for copy in first_halos:
         copy.start()
 
     pair_c[1].wait_recv()
@@ -230,6 +264,8 @@
         upper_x = (jnp.where(last_lane, high_rolled, low_rolled), jnp.where(last_lane, edge, high_rolled))
         before = []
         after = []
+        inverses = []
+        uppers = []
         for j, part in enumerate(halves):
             here_y = by[z, :, part]
             upper_y = jnp.where(
@@ -240,6 +276,11 @@
             for face in faces:
                 centre = centre + face
             inverse = 1.0 / centre
+            inverses.append(inverse)
+            inverse_ref[z, :, part] = inverse
+            sent_y[0, 0, 2, z, :, part] = inverse[:1]
+            sent_y[0, 1, 2, z, :, part] = inverse[NY - 1 :]
+            uppers.append(upper_y[NY - ROWS :])
             diag[z, :, part] = centre
             scaled[z, :, part] = inverse * rhs[z, :, part]
             weights = [inverse * face for face in faces]
@@ -255,18 +296,47 @@
             weights[3] = jnp.where(end_row, 0.0, weights[3])
             for i, weight in enumerate(weights):
                 near[i, z, :, part] = weight
+        edge_pack, inverse_pack, y_pack = carry
         for g, rows in enumerate(group_rows):
-            carry = packed(z, g, before[0][rows], after[1][rows], carry)
-        return carry
-
-    edge_x[...] = planes(scale_body, zero_pack)
-
-    def inner(k, z, first, last):
+            edge_pack = packed(z, g, before[0][rows], after[1][rows], edge_pack)
+            inverse_pack = packed(z, g, inverses[0][rows], inverses[1][rows], inverse_pack)
+        y_pack = packed(z, 0, by[z, :ROWS, :LANES], by[z, :ROWS, LANES:], y_pack)
+        y_pack = packed(z, GROUPS - 1, uppers[0], uppers[1], y_pack)
+        return edge_pack, inverse_pack, y_pack
+
+    edge_x[...], sent_x[0, 2], y_pack = planes(scale_body, (zero_pack, zero_pack, zero_pack))
+    odd = lane8 - 2 * spots == 1
+    spot_group = spots - GROUPS * (spots // GROUPS)
+    low_rim = (spot_group == 0) & (row8 == 0)
+    high_rim = (spot_group == GROUPS - 1) & (row8 == ROWS - 1)
+    low_spots = spots < GROUPS
+    high_spots = (spots >= GROUPS * (NZ - 1)) & (spots < GROUPS * NZ)
+    z_pack = zero_pack
+    for g, rows in enumerate(group_rows):
+        z_pack = packed(0, g, bz[0, rows, :LANES], bz[0, rows, LANES:], z_pack)
+        z_pack = packed(NZ - 1, g, bz[NZ, rows, :LANES], bz[NZ, rows, LANES:], z_pack)
+    beta_pack[0] = jnp.where(odd, rim_pack[...], pltpu.roll(rim_values, LANES - 1, 1))
+    beta_pack[1] = jnp.where(low_rim | high_rim, y_pack, 0.0)
+    beta_pack[2] = z_pack
+    sent_z[0, 0, 2] = inverse_ref[0]
+    sent_z[0, 1, 2] = inverse_ref[NZ - 1]
+
+    def swapped(value):
+        return jnp.where(odd, pltpu.roll(value, 1, 1), pltpu.roll(value, LANES - 1, 1))
+
+    def halo_z_of(k, side):
+        return got_z.at[k // 2, side, 0] if k % 2 else field.at[k, side * (NZ + 1)]
+
+    def halo_y_of(k, side):
+        return got_y.at[k // 2, side, 0] if k % 2 else halo_y.at[k, side]
+
+    def inner(k, z, first, last, carry):
         low, high = field[k, z + 1, :, :LANES], field[k, z + 1, :, LANES:]
         low_after, high_after = pltpu.roll(low, LANES - 1, 1), pltpu.roll(high, LANES - 1, 1)
         low_before, high_before = pltpu.roll(low, 1, 1), pltpu.roll(high, 1, 1)
         x_before = (low_before, jnp.where(first_lane, low_before, high_before))
         x_after = (jnp.where(last_lane, high_after, low_after), high_after)
+        values = []
         for j, part in enumerate(halves):
             here = (low, high)[j]
             value = scaled[z, :, part] - here
@@ -278,21 +348,39 @@
             if not last:
                 value = value + near[5, z, :, part] * field[k, z + 2, :, part]
             scaled[z, :, part] = value
+            values.append(value)
+            if k % 2:
+                ahead = SECOND[k] * value + FIRST[k] * here
+                sent_y[k // 2, 0, 1, z, :, part] = ahead[:1]
+                sent_y[k // 2, 1, 1, z, :, part] = ahead[NY - 1 :]
+                if first:
+                    sent_z[k // 2, 0, 1, :, part] = ahead
+                if last:
+                    sent_z[k // 2, 1, 1, :, part] = ahead
+        if k % 2:
+            for g, rows in enumerate(group_rows):
+                carry = packed(z, g, values[0][rows], values[1][rows], carry)
+        return carry
 
     def outer(k, z, first, last, sides, carry):
         fresh = [[], []]
+        sending = k % 2 == 0 and k < SWEEPS
         for g, rows in enumerate(group_rows):
             moved = pltpu.roll(sides, LANES - 1 - 2 * (z * GROUPS + g), 1)
             for j, part in enumerate(halves):
                 value = scaled[z, rows, part] + jnp.where(lane8 == (0, LANES - 1)[j], moved, 0.0)
                 if g == 0:
-                    value = value + edge_y[0, z, :, part] * jnp.broadcast_to(halo_y[k, 0, z, :, part], (ROWS, LANES))
+                    value = value + edge_y[0, z, :, part] * jnp.broadcast_to(
+                        halo_y_of(k, 0)[z, :, part], (ROWS, LANES)
+                    )
                 if g == GROUPS - 1:
-                    value = value + edge_y[1, z, :, part] * jnp.broadcast_to(halo_y[k, 1, z, :, part], (ROWS, LANES))
+                    value = value + edge_y[1, z, :, part] * jnp.broadcast_to(
+                        halo_y_of(k, 1)[z, :, part], (ROWS, LANES)
+                    )
                 if first:
-                    value = value + near[4, z, rows, part] * field[k, z, rows, part]
+                    value = value + near[4, z, rows, part] * halo_z_of(k, 0)[rows, part]
                 if last:
-                    value = value + near[5, z, rows, part] * field[k, z + 2, rows, part]
+                    value = value + near[5, z, rows, part] * halo_z_of(k, 1)[rows, part]
                 if k == SWEEPS:
                     resid[z, rows, part] = diag[z, rows, part] * value
                     continue
@@ -301,48 +389,145 @@
                 if k > 0:
                     step = step + FIRST[k] * field[k, z + 1, rows, part]
                 field[k + 1, z + 1, rows, part] = step
-                total[z, rows, part] = total[z, rows, part] + step
+                if k == SWEEPS - 1:
+                    total[z, rows, part] = total[z, rows, part] + step
+                if not sending:
+                    continue
+                if first:
+                    sent_z[k // 2, 0, 0, rows, part] = step
+                if last:
+                    sent_z[k // 2, 1, 0, rows, part] = step
                 if g == 0:
-                    face_y[k + 1, 0, z, :, part] = step[0:1, :]
+                    sent_y[k // 2, 0, 0, z, :, part] = step[:1]
                 if g == GROUPS - 1:
-                    face_y[k + 1, 1, z, :, part] = step[ROWS - 1 : ROWS, :]
+                    sent_y[k // 2, 1, 0, z, :, part] = step[ROWS - 1 :]
                 fresh[j].append(step)
-            if k < SWEEPS:
+            if sending:
                 carry = packed(z, g, fresh[0][g], fresh[1][g], carry)
         return carry
 
-    def apply(k):
-        inner(k, 0, True, False)
-
-        def inner_body(z, carry):
-            inner(k, z, False, False)
-            return carry
-
-        planes(inner_body, 0, 1, NZ - 1)
-        inner(k, NZ - 1, False, True)
-        for copy in halos[k]:
-            copy.wait_recv()
-        from_low = pltpu.roll(halo_x[k, 0], 1, 1)
-        from_high = pltpu.roll(halo_x[k, 1], LANES - 1, 1)
-        sides = edge_x[...] * jnp.where(lane8 - 2 * spots == 1, from_low, from_high)
+    def run_inner(k):
+        carry = inner(k, 0, True, False, zero_pack)
+        carry = planes(lambda z, carry: inner(k, z, False, False, carry), carry, 1, NZ - 1)
+        return inner(k, NZ - 1, False, True, carry)
+
+    def run_outer(k, x_halo):
+        sides = edge_x[...] * swapped(x_halo)
         carry = outer(k, 0, True, False, sides, zero_pack)
         carry = planes(lambda z, carry: outer(k, z, False, False, sides, carry), carry, 1, NZ - 1)
         return outer(k, NZ - 1, False, True, sides, carry)
 
-    for k in range(SWEEPS):
-        pack[k + 1] = apply(k)
-        for copy in halos[k + 1]:
+    def spread_low(source, spot):
+        return pltpu.roll(source, (LANES - 2 * spot) % LANES, 1)
+
+    def spread_high(source, spot):
+        return pltpu.roll(source, 126 - 2 * spot, 1)
+
+    def ahead_z(r, k, side):
+        own = side * (NZ - 1)
+        sender = NZ - 1 - own
+        for j, part in enumerate(halves):
+            value = bz[side * NZ, :, part] * field[k, own + 1, :, part]
+            for b, at in ((0, 0), (1, NY - 1)):
+                line = jnp.broadcast_to(got_yz[r, side, b, 0, :, part], (NY, LANES))
+                value = value + jnp.where(row == at, line, 0.0)
+            source = got_xz[r, j, side, 0]
+            move = (spread_low, spread_high)[j]
+            column = jnp.concatenate([move(source, sender * GROUPS + g) for g in range(GROUPS)], axis=0)
+            value = value + jnp.where((first_lane, last_lane)[j], column, 0.0)
+            value = got_z[r, side, 1, :, part] + SECOND[k] * got_z[0, side, 2, :, part] * value
+            field[k + 1, side * (NZ + 1), :, part] = value
+
+    def ahead_y(r, k, side):
+        sender_group = (GROUPS - 1) * (1 - side)
+        sender_row = (ROWS - 1) * (1 - side)
+        face = (rim_face, rim_y)[side]
+        sources = [got_xy[r, j, side, 0] for j in range(2)]
+        for z in range(NZ):
+            for j, part in enumerate(halves):
+                value = face[z, :, part] * sent_y[r, side, 0, z, :, part]
+                if z == 0:
+                    value = value + got_yz[r, 0, side, 1, :, part]
+                if z == NZ - 1:
+                    value = value + got_yz[r, 1, side, 1, :, part]
+                column = (spread_low, spread_high)[j](sources[j], z * GROUPS + sender_group)
+                column = jnp.where(lane8 == (0, LANES - 1)[j], column, 0.0)
+                value = value + column[sender_row : sender_row + 1]
+                value = got_y[r, side, 1, z, :, part] + SECOND[k] * got_y[0, side, 2, z, :, part] * value
+                halo_y[k + 1, side, z, :, part] = value
+
+    def either(ref_low, ref_high):
+        return jnp.where(odd, ref_high, ref_low)
+
+    def ahead_x(r, k):
+        value = swapped(sent_q[r, 0])
+        below = either(got_xy[r, 0, 0, 1], got_xy[r, 1, 0, 1])
+        above = either(got_xy[r, 0, 1, 1], got_xy[r, 1, 1, 1])
+        shift = 2 * (GROUPS - 1)
+        value = value + jnp.where(low_rim, pltpu.roll(pltpu.roll(below, 1, 0), LANES - shift, 1), 0.0)
+        value = value + jnp.where(high_rim, pltpu.roll(pltpu.roll(above, ROWS - 1, 0), shift, 1), 0.0)
+        below = either(got_xz[r, 0, 0, 2], got_xz[r, 1, 0, 2])
+        above = either(got_xz[r, 0, 1, 2], got_xz[r, 1, 1, 2])
+        shift = 2 * GROUPS * (NZ - 1)
+        value = value + jnp.where(low_spots, pltpu.roll(below, LANES - shift, 1), 0.0)
+        value = value + jnp.where(high_spots, pltpu.roll(above, shift, 1), 0.0)
+        partial = either(got_x[r, 0, 1], got_x[r, 1, 1])
+        return partial + SECOND[k] * either(got_x[0, 0, 2], got_x[0, 1, 2]) * value
+
+    def apply_two(r):
+        k = 2 * r + 1
+        own = sent_x[r, 0]
+        for i in range(3):
+            sent_q[r, i] = beta_pack[i] * own
+        for a in range(2):
+            z = a * (NZ - 1)
+            for b in range(2):
+                line = sent_y[r, b, 0, z]
+                at = b * (NY - 1)
+                sent_yz[r, a, b, 0] = (rim_face, rim_y)[b][z] * line
+                sent_yz[r, a, b, 1] = bz[a * NZ, at : at + 1, :] * line
+        copies = edge_copies(r)
+        for copy in copies:
             copy.start()
+        sent_x[r, 1] = SECOND[k] * run_inner(k) + FIRST[k] * own
+        more = face_copies(r)
+        for copy in more:
+            copy.start()
+
+        def sum_body(z, carry):
+            for part in halves:
+                if r == 0:
+                    total[z, :, part] = field[0, z + 1, :, part] + field[1, z + 1, :, part]
+                else:
+                    total[z, :, part] = (
+                        total[z, :, part] + field[2, z + 1, :, part] + field[3, z + 1, :, part]
+                    )
+            return carry
+
+        planes(sum_body)
+        for copy in copies + more:
+            copy.wait_recv()
+        run_outer(k, either(got_x[r, 0, 0], got_x[r, 1, 0]))
+        if k == SWEEPS - 1:
+            x_out.start()
+        x_halo = ahead_x(r, k)
+        for side in range(2):
+            ahead_z(r, k, side)
+            ahead_y(r, k, side)
+        run_inner(k + 1)
+        return copies + more, run_outer(k + 1, x_halo)
+
     x_out = pltpu.make_async_copy(total, x_hbm, out_sem.at[0])
-    x_out.start()
-    apply(SWEEPS)
+    run_inner(0)
+    for copy in first_halos:
+        copy.wait_recv()
+    sent_x[0, 0] = run_outer(0, either(halo_x[0, 0], halo_x[0, 1]))
+    first_copies, sent_x[1, 0] = apply_two(0)
+    second_copies, unused = apply_two(1)
     r_out = pltpu.make_async_copy(resid, r_hbm, out_sem.at[1])
     r_out.start()
-    for copy in pair_f + pair_c + rims:
+    for copy in pair_f + pair_c + rims + first_halos + first_copies + second_copies:
         copy.wait_send()
-    for copies in halos:
-        for copy in copies:
-            copy.wait_send()
     x_out.wait()
     r_out.wait()
 
@@ -365,7 +550,7 @@
     dma = pltpu.SemaphoreType.DMA
     anywhere = pl.BlockSpec(memory_space=pl.ANY)
     hbm = pl.BlockSpec(memory_space=pltpu.HBM)
-    held = jnp.transpose(held_slabs, (1, 2, 0))
+    held = pltpu.with_memory_space_constraint(jnp.transpose(held_slabs, (1, 2, 0)), pltpu.HBM)
     results = pl.pallas_call(
         kernel,
         out_shape=(jax.ShapeDtypeStruct(brick, F32), jax.ShapeDtypeStruct(brick, F32)),
@@ -391,6 +576,7 @@
             pltpu.VMEM(brick, F32),
             pltpu.VMEM(brick, F32),
             pltpu.VMEM(brick, F32),
+            pltpu.VMEM(brick, F32),
             pltpu.VMEM((rounds, ROWS, LANES), F32),
             pltpu.VMEM((rounds, 2, NZ, 1, NX), F32),
             pltpu.VMEM((rounds, 2, ROWS, LANES), F32),
@@ -399,6 +585,18 @@
             pltpu.VMEM((NZ, 1, NX), F32),
             pltpu.VMEM((ROWS, LANES), F32),
             pltpu.VMEM((NZ, 1, NX), F32),
+            pltpu.VMEM((3, ROWS, LANES), F32),
+            pltpu.VMEM((2, 2, 3, NY, NX), F32),
+            pltpu.VMEM((2, 2, 3, NY, NX), F32),
+            pltpu.VMEM((2, 2, 3, NZ, 1, NX), F32),
+            pltpu.VMEM((2, 2, 3, NZ, 1, NX), F32),
+            pltpu.VMEM((2, 3, ROWS, LANES), F32),
+            pltpu.VMEM((2, 2, 3, ROWS, LANES), F32),
+            pltpu.VMEM((2, 2, 2, 2, 1, NX), F32),
+            pltpu.VMEM((2, 2, 2, 2, 1, NX), F32),
+            pltpu.VMEM((2, 3, ROWS, LANES), F32),
+            pltpu.VMEM((2, 2, 2, 3, ROWS, LANES), F32),
+            pltpu.VMEM((2, 2, 2, 3, ROWS, LANES), F32),
             pltpu.SMEM((1, 1, slots), jnp.int32),
             dma((6,)),
             dma((1,)),
@@ -409,6 +607,8 @@
             dma((3,)),
             dma((3,)),
             dma((2,)),
+            dma((2, 18)),
+            dma((2, 18)),
         ],
         compiler_params=pltpu.CompilerParams(
             collective_id=0, has_side_effects=True, vmem_limit_bytes=55767040

time: 33.7 us -> 34 us (level); the launches traced: 33.1 us -> 33.9 us
  Pallas kernels: 31.8 us -> 33.3 us
  local copies, waits for them, and re-layouts: 0.65 us -> 0 us
    pallas_call x1, Pallas kernels: 30.9 us -> 32.4 us  [local(): pl.pallas_call(kernel, out_shape=(jax.ShapeDtypeStruct(brick, F32), jax.S...]
    unnamed x2 -> x0, local copies, waits for them, and re-layouts: 0.65 us -> none
where the time goes in v3:
time: 34 us; the launch traced here: 33.9 us
  Pallas kernels  33.3 us (98%)
  between operations  0.64 us (2%)
    pallas_call x1, Pallas kernels, local(): pl.pallas_call(kernel, out_shape=(jax.ShapeDtypeStruct(brick, F32), jax.S...  32.4 us
    pallas_call x1, Pallas kernels, local(): pl.pallas_call(emit, out_shape=(jax.ShapeDtypeStruct(brick, F32), jax.Sha...  0.89 us

profile of v3, /device:TPU:1, one launch (start us, length us, event | category | flops | bytes accessed | tf_op | source)
XLA Modules:
  0.0 33.9 jit_solution(7700037098534602735)
XLA Ops:
  0.6 32.4 %smooth.1 = (f32[16,24,256]{2,1,0:T(8,128)S(1)}, f32[16,24,256]{2,1,0:T(8,128)S(1)}) custom-call(f32[2,2,16,2,8,256]{5,4,3,2,1,0:T(8,128)} %bitcast.3, bf16[4,2,16,2,8,256]{5,4,3,2,1,0:T(8,128)(2,1)} %bitcast.4, s32[1,1,2]{2,1,0:T(1,128)} %bitcast.5), custom_call_target="tpu_custom_call" | custom-call | tf_op jit(solution)/shard_map/smooth/pallas_call | solution.py:554
  33.0 0.9 %emit.1 = (f32[16,24,256]{2,1,0:T(8,128)}, f32[16,24,256]{2,1,0:T(8,128)}) custom-call(f32[16,24,256]{2,1,0:T(8,128)S(1)} %get-tuple-element.4.x_ref, f32[16,24,256]{2,1,0:T(8,128)S(1)} %get-tuple-element.5.r_ref), custom_call_target="tpu_custom_call" | custom-call | tf_op jit(solution)/shard_map/emit/pallas_call | solution.py:618

commit v4 on v2

--- a/solution.py
+++ b/solution.py
@@ -50,8 +50,9 @@
     fields_hbm, coef_hbm, held_hbm, x_hbm, r_hbm,
     slots_f, slots_c, send_f, send_c, recv_f, recv_c,
     field, alpha, bx, by, bz, rhs, near, edge_y, edge_x, diag, scaled, total, resid,
-    pack, face_y, halo_x, halo_y, rim_pack, rim_face, rim_x, rim_y, held_ref,
-    load_sem, held_sem, pair_send, pair_recv, halo_send, halo_recv, rim_send, rim_recv, out_sem,
+    pack, face_y, halo_x, halo_y, rim_y, held_ref,
+    part_x, part_y, part_z, part_p, inner_y, got_x, got_y, got_z, got_p,
+    load_sem, held_sem, pair_send, pair_recv, halo_send, halo_recv, part_send, got_sem, out_sem,
 ):
     group = lax.axis_index("gy")
     half = lax.rem(group, 2)
@@ -62,7 +63,12 @@
     z_low, z_high = ring("gz")
 
     barrier = pltpu.get_barrier_semaphore()
-    for neighbour in (x_low, x_high, y_low, y_high, z_low, z_high):
+    devices = lax.axis_size("gy")
+    pair = [{"gy": group - half}, {"gy": group - half + 1}]
+    outer_first = lax.rem(group - half + devices + 4 * half - 2, devices)
+    fans = [{**side, **member} for side in (x_low, x_high, z_low, z_high) for member in pair]
+    callers = fans + [{"gy": outer_first}, {"gy": outer_first + 1}, partner]
+    for neighbour in callers:
         pl.semaphore_signal(barrier, inc=1, device_id=neighbour, device_id_type=MESH)
 
     load_held = pltpu.make_async_copy(held_hbm, held_ref, held_sem.at[0])
@@ -104,20 +110,32 @@
 
     def halo_copies(k):
         return [
+            copy_to(pack.at[k], halo_x.at[k, 1], halo_send.at[k, 0], halo_recv.at[k, 0], x_low),
+            copy_to(pack.at[k], halo_x.at[k, 0], halo_send.at[k, 1], halo_recv.at[k, 1], x_high),
+            copy_to(face_y.at[k, 0], halo_y.at[k, 1], halo_send.at[k, 2], halo_recv.at[k, 2], y_low),
+            copy_to(face_y.at[k, 1], halo_y.at[k, 0], halo_send.at[k, 3], halo_recv.at[k, 3], y_high),
             copy_to(field.at[k, 1], field.at[k, NZ + 1], halo_send.at[k, 4], halo_recv.at[k, 4], z_low),
             copy_to(field.at[k, NZ], field.at[k, 0], halo_send.at[k, 5], halo_recv.at[k, 5], z_high),
-            copy_to(face_y.at[k, 0], halo_y.at[k, 1], halo_send.at[k, 2], halo_recv.at[k, 2], y_low),
-            copy_to(face_y.at[k, 1], halo_y.at[k, 0], halo_send.at[k, 3], halo_recv.at[k, 3], y_high),
-            copy_to(pack.at[k], halo_x.at[k, 1], halo_send.at[k, 0], halo_recv.at[k, 0], x_low),
-            copy_to(pack.at[k], halo_x.at[k, 0], halo_send.at[k, 1], halo_recv.at[k, 1], x_high),
         ]
 
-    halos = [halo_copies(k) for k in range(SWEEPS + 1)]
-    rims = [
-        copy_to(rim_pack, rim_x, rim_send.at[0], rim_recv.at[0], x_low),
-        copy_to(rim_face, rim_y, rim_send.at[1], rim_recv.at[1], y_low),
-        copy_to(bz.at[0], bz.at[NZ], rim_send.at[2], rim_recv.at[2], z_low),
-    ]
+    halos = [None] + [halo_copies(k) for k in range(1, SWEEPS + 1)]
+    def part_copy(i, slot, source, target, device):
+        return copy_to(source, target, part_send.at[i], got_sem.at[slot, half], device)
+
+    parts = []
+    for h, member in enumerate(pair):
+        parts.append(part_copy(h, 1, part_x.at[h], got_x.at[1, half], {**x_low, **member}))
+    for h, member in enumerate(pair):
+        parts.append(part_copy(2 + h, 0, part_x.at[h], got_x.at[0, half], {**x_high, **member}))
+    parts.append(part_copy(4, 4, part_y.at[0], got_y.at[half], {"gy": lax.rem(group - half + devices - 1, devices)}))
+    parts.append(part_copy(5, 4, part_y.at[1], got_y.at[half], {"gy": lax.rem(group - half + 2, devices)}))
+    for h, member in enumerate(pair):
+        parts.append(part_copy(6 + h, 3, part_z.at[0, h], got_z.at[1, half], {**z_low, **member}))
+    for h, member in enumerate(pair):
+        parts.append(
+            part_copy(8 + h, 2, part_z.at[1, h, pl.ds(0, 1)], got_z.at[0, half, pl.ds(0, 1)], {**z_high, **member})
+        )
+    parts.append(copy_to(part_p, got_p, part_send.at[10], pair_recv.at[6], partner))
 
     def planes(body, carry=0, first=0, last=NZ):
         return lax.fori_loop(first, last, body, carry, unroll=True)
@@ -138,17 +156,85 @@
         ).astype(F32)
 
     def packed(z, g, tile_low, tile_high, carry):
-        spot = z * GROUPS + g
+        return packed_at(g * NZ + z, tile_low, tile_high, carry)
+
+    def packed_at(spot, tile_low, tile_high, carry):
         both = jnp.where(lane8 == 0, tile_low, tile_high)
-        moved = pltpu.roll(both, 2 * spot + 1, 1)
+        moved = pltpu.roll(both, (2 * spot + 1) % LANES, 1)
         return jnp.where(spots == spot, moved, carry)
+
+    region = [first_slab + g // 2 for g in range(2 * GROUPS)]
+
+    def chosen(slab, first, second):
+        zero = jnp.zeros(first.shape, first.dtype)
+        return lax.select(id0 == slab, first, lax.select(id1 == slab, second, zero)).astype(F32)
+
+    def part_columns(slots, index):
+        def body(z, carry):
+            for slot in range(2):
+                for p in range(2):
+                    value = slots[slot, z, p].astype(F32)
+                    carry = packed_at((2 * slot + p) * NZ + z, value[:, :LANES], value[:, LANES:], carry)
+            return carry
+
+        whole = planes(body, jnp.zeros((ROWS, LANES), F32))
+        segment = LANES // 4
+        for h in range(2):
+            value = jnp.zeros((ROWS, LANES), F32)
+            for g in range(GROUPS):
+                p = (GROUPS * h + g) % 2
+                moved = [pltpu.roll(whole, segment * (g - 2 * slot - p) % LANES, 1) for slot in range(2)]
+                value = jnp.where(lane8 // segment == g, chosen(region[GROUPS * h + g], *moved), value)
+            part_x[h, index] = value
+
+    def part_planes(slots, side, index):
+        z = side * (NZ - 1)
+        for g in range(2 * GROUPS):
+            rows = slice((g % GROUPS) * ROWS, (g % GROUPS + 1) * ROWS)
+            part_z[side, g // GROUPS, index, rows, :] = chosen(region[g], slots[0, z, g % 2], slots[1, z, g % 2])
+
+    def part_rows(slots, index):
+        middle = first_slab + 1
+
+        def body(z, carry):
+            part_y[0, index, z] = chosen(region[0], slots[0, z, 0, 0:1], slots[1, z, 0, 0:1])
+            part_y[1, index, z] = chosen(region[5], slots[0, z, 1, ROWS - 1 : ROWS], slots[1, z, 1, ROWS - 1 : ROWS])
+            upper = chosen(middle, slots[0, z, 1, 0:1], slots[1, z, 1, 0:1])
+            lower = chosen(middle, slots[0, z, 0, ROWS - 1 : ROWS], slots[1, z, 0, ROWS - 1 : ROWS])
+            part_p[index, z] = lax.select(half == 0, lower, upper)
+            inner_y[index, z] = lax.select(half == 0, upper, lower)
+            return carry
+
+        planes(body)
+
+    def plain(slots, received, out, shift=0):
+        def body(z, carry):
+            for g in range(GROUPS):
+                out[z + shift, g * ROWS : (g + 1) * ROWS, :] = assembled(slots, received, z, g)
+            return carry
+
+        planes(body)
 
     loads_f[0].wait()
     prepare(slots_f.at[0], send_f.at[0])
-    pl.semaphore_wait(barrier, 6)
+    part_columns(slots_f.at[0], 0)
+    part_rows(slots_f.at[0], 0)
+    part_planes(slots_f.at[0], 0, 0)
+    part_planes(slots_f.at[0], 1, 0)
+    loads_c[1].wait()
+    part_columns(slots_c.at[1], 1)
+    loads_c[2].wait()
+    part_rows(slots_c.at[2], 1)
+    loads_c[3].wait()
+    part_planes(slots_c.at[3], 0, 1)
+    pl.semaphore_wait(barrier, len(callers))
+    for copy in parts[:10]:
+        copy.start()
     pair_f[0].start()
     for c in (1, 2, 3, 0):
-        loads_c[c].wait()
+        if c == 0:
+            parts[10].start()
+            loads_c[c].wait()
         prepare(slots_c.at[c], send_c.at[c])
         pair_c[c].start()
     loads_f[1].wait()
@@ -158,74 +244,54 @@
     zero_pack = jnp.zeros((ROWS, LANES), F32)
 
     pair_f[0].wait_recv()
-
-    def start_body(z, carry):
-        for g in range(GROUPS):
-            value = assembled(slots_f.at[0], recv_f.at[0], z, g)
-            field[0, z + 1, g * ROWS : (g + 1) * ROWS, :] = value
-            total[z, g * ROWS : (g + 1) * ROWS, :] = value
-            if g == 0:
-                face_y[0, 0, z] = value[0:1, :]
-            if g == GROUPS - 1:
-                face_y[0, 1, z] = value[ROWS - 1 : ROWS, :]
-            carry = packed(z, g, value[:, :LANES], value[:, LANES:], carry)
+    plain(slots_f.at[0], recv_f.at[0], field.at[0], 1)
+
+    def sum_body(z, carry):
+        total[z] = field[0, z + 1]
         return carry
 
-    pack[0] = planes(start_body, zero_pack)
-    for copy in halos[0]:
-        copy.start()
-
+    planes(sum_body)
     pair_c[1].wait_recv()
-
-    def bx_body(z, carry):
-        for g in range(GROUPS):
-            value = assembled(slots_c.at[1], recv_c.at[1], z, g)
-            bx[z, g * ROWS : (g + 1) * ROWS, :] = value
-            carry = packed(z, g, value[:, :LANES], value[:, LANES:], carry)
-        return carry
-
-    rim_pack[...] = planes(bx_body, zero_pack)
-    rims[0].start()
+    plain(slots_c.at[1], recv_c.at[1], bx)
     pair_c[2].wait_recv()
-
-    def by_body(z, carry):
-        for g in range(GROUPS):
-            value = assembled(slots_c.at[2], recv_c.at[2], z, g)
-            by[z, g * ROWS : (g + 1) * ROWS, :] = value
-            if g == 0:
-                rim_face[z] = value[0:1, :]
-        return carry
-
-    planes(by_body)
-    rims[1].start()
-
-    def plain(slots, received, out):
-        def body(z, carry):
-            for g in range(GROUPS):
-                out[z, g * ROWS : (g + 1) * ROWS, :] = assembled(slots, received, z, g)
-            return carry
-
-        planes(body)
-
+    plain(slots_c.at[2], recv_c.at[2], by)
     pair_c[3].wait_recv()
     plain(slots_c.at[3], recv_c.at[3], bz)
-    rims[2].start()
     pair_c[0].wait_recv()
     plain(slots_c.at[0], recv_c.at[0], alpha)
     pair_f[1].wait_recv()
     plain(slots_f.at[1], recv_f.at[1], rhs)
-    for copy in rims:
-        copy.wait_recv()
+    parts[10].wait_recv()
+    for member in range(2):
+        for side in range(2):
+            copy_to(part_x.at[0], got_x.at[side, member], part_send.at[0], got_sem.at[side, member], x_low).wait_recv()
+            count = pl.ds(0, 1 + side)
+            source, target = part_z.at[0, 0, count], got_z.at[side, member, count]
+            copy_to(source, target, part_send.at[0], got_sem.at[2 + side, member], z_low).wait_recv()
+        copy_to(part_y.at[0], got_y.at[member], part_send.at[0], got_sem.at[4, member], y_low).wait_recv()
+
+    for side in range(2):
+        halo_x[0, side] = got_x[side, 0, 0] + got_x[side, 1, 0]
+        field[0, side * (NZ + 1)] = got_z[side, 0, 0] + got_z[side, 1, 0]
+    bz[NZ] = got_z[1, 0, 1] + got_z[1, 1, 1]
+    rim_values = got_x[1, 0, 1] + got_x[1, 1, 1]
+
+    def row_body(z, carry):
+        halo_y[0, half, z] = got_y[0, 0, z] + got_y[1, 0, z]
+        halo_y[0, 1 - half, z] = inner_y[0, z] + got_p[0, z]
+        rim_y[z] = lax.select(half == 0, inner_y[1, z] + got_p[1, z], got_y[0, 1, z] + got_y[1, 1, z])
+        return carry
+
+    planes(row_body)
 
     halves = (slice(0, LANES), slice(LANES, NX))
     group_rows = [slice(g * ROWS, (g + 1) * ROWS) for g in range(GROUPS)]
-    rim_values = rim_x[...]
 
     def scale_body(z, carry):
         low_rolled = pltpu.roll(bx[z, :, :LANES], LANES - 1, 1)
         high_rolled = pltpu.roll(bx[z, :, LANES:], LANES - 1, 1)
         edge = jnp.concatenate(
-            [pltpu.roll(rim_values, 126 - 2 * (z * GROUPS + g), 1) for g in range(GROUPS)], axis=0
+            [pltpu.roll(rim_values, 126 - 2 * (g * NZ + z), 1) for g in range(GROUPS)], axis=0
         )
         upper_x = (jnp.where(last_lane, high_rolled, low_rolled), jnp.where(last_lane, edge, high_rolled))
         before = []
@@ -282,7 +348,7 @@
     def outer(k, z, first, last, sides, carry):
         fresh = [[], []]
         for g, rows in enumerate(group_rows):
-            moved = pltpu.roll(sides, LANES - 1 - 2 * (z * GROUPS + g), 1)
+            moved = pltpu.roll(sides, LANES - 1 - 2 * (g * NZ + z), 1)
             for j, part in enumerate(halves):
                 value = scaled[z, rows, part] + jnp.where(lane8 == (0, LANES - 1)[j], moved, 0.0)
                 if g == 0:
@@ -320,8 +386,9 @@
 
         planes(inner_body, 0, 1, NZ - 1)
         inner(k, NZ - 1, False, True)
-        for copy in halos[k]:
-            copy.wait_recv()
+        if k > 0:
+            for copy in halos[k]:
+                copy.wait_recv()
         from_low = pltpu.roll(halo_x[k, 0], 1, 1)
         from_high = pltpu.roll(halo_x[k, 1], LANES - 1, 1)
         sides = edge_x[...] * jnp.where(lane8 - 2 * spots == 1, from_low, from_high)
@@ -338,9 +405,9 @@
     apply(SWEEPS)
     r_out = pltpu.make_async_copy(resid, r_hbm, out_sem.at[1])
     r_out.start()
-    for copy in pair_f + pair_c + rims:
+    for copy in pair_f + pair_c + parts:
         copy.wait_send()
-    for copies in halos:
+    for copies in halos[1:]:
         for copy in copies:
             copy.wait_send()
     x_out.wait()
@@ -365,7 +432,7 @@
     dma = pltpu.SemaphoreType.DMA
     anywhere = pl.BlockSpec(memory_space=pl.ANY)
     hbm = pl.BlockSpec(memory_space=pltpu.HBM)
-    held = jnp.transpose(held_slabs, (1, 2, 0))
+    held = pltpu.with_memory_space_constraint(jnp.transpose(held_slabs, (1, 2, 0)), pltpu.HBM)
     results = pl.pallas_call(
         kernel,
         out_shape=(jax.ShapeDtypeStruct(brick, F32), jax.ShapeDtypeStruct(brick, F32)),
@@ -395,19 +462,25 @@
             pltpu.VMEM((rounds, 2, NZ, 1, NX), F32),
             pltpu.VMEM((rounds, 2, ROWS, LANES), F32),
             pltpu.VMEM((rounds, 2, NZ, 1, NX), F32),
-            pltpu.VMEM((ROWS, LANES), F32),
-            pltpu.VMEM((NZ, 1, NX), F32),
-            pltpu.VMEM((ROWS, LANES), F32),
             pltpu.VMEM((NZ, 1, NX), F32),
             pltpu.SMEM((1, 1, slots), jnp.int32),
+            pltpu.VMEM((2, 2, ROWS, LANES), F32),
+            pltpu.VMEM((2, 2, NZ, 1, NX), F32),
+            pltpu.VMEM((2, 2, 2, NY, NX), F32),
+            pltpu.VMEM((2, NZ, 1, NX), F32),
+            pltpu.VMEM((2, NZ, 1, NX), F32),
+            pltpu.VMEM((2, 2, 2, ROWS, LANES), F32),
+            pltpu.VMEM((2, 2, NZ, 1, NX), F32),
+            pltpu.VMEM((2, 2, 2, NY, NX), F32),
+            pltpu.VMEM((2, NZ, 1, NX), F32),
             dma((6,)),
             dma((1,)),
             dma((6,)),
-            dma((6,)),
+            dma((7,)),
             dma((rounds, 6)),
             dma((rounds, 6)),
-            dma((3,)),
-            dma((3,)),
+            dma((11,)),
+            dma((5, 2)),
             dma((2,)),
         ],
         compiler_params=pltpu.CompilerParams(

time: 33.7 us -> 33.1 us (0.982)
  local copies, waits for them, and re-layouts: 0.65 us -> 0 us
    unnamed x2 -> x0, local copies, waits for them, and re-layouts: 0.65 us -> none
where the time goes in v4:
time: 33.1 us; the launch traced here: 32.7 us
  Pallas kernels  32.1 us (97%)
  between operations  0.64 us (2%)
    pallas_call x1, Pallas kernels, local(): pl.pallas_call(kernel, out_shape=(jax.ShapeDtypeStruct(brick, F32), jax.S...  31.2 us
    pallas_call x1, Pallas kernels, local(): pl.pallas_call(emit, out_shape=(jax.ShapeDtypeStruct(brick, F32), jax.Sha...  0.89 us

profile of v4, /device:TPU:1, one launch (start us, length us, event | category | flops | bytes accessed | tf_op | source)
XLA Modules:
  0.0 32.7 jit_solution(11160529430241057405)
XLA Ops:
  0.6 31.2 %smooth.1 = (f32[16,24,256]{2,1,0:T(8,128)S(1)}, f32[16,24,256]{2,1,0:T(8,128)S(1)}) custom-call(f32[2,2,16,2,8,256]{5,4,3,2,1,0:T(8,128)} %bitcast.3, bf16[4,2,16,2,8,256]{5,4,3,2,1,0:T(8,128)(2,1)} %bitcast.4, s32[1,1,2]{2,1,0:T(1,128)} %bitcast.5), custom_call_target="tpu_custom_call" | custom-call | tf_op jit(solution)/shard_map/smooth/pallas_call | solution.py:436
  31.8 0.9 %emit.1 = (f32[16,24,256]{2,1,0:T(8,128)}, f32[16,24,256]{2,1,0:T(8,128)}) custom-call(f32[16,24,256]{2,1,0:T(8,128)S(1)} %get-tuple-element.4.x_ref, f32[16,24,256]{2,1,0:T(8,128)S(1)} %get-tuple-element.5.r_ref), custom_call_target="tpu_custom_call" | custom-call | tf_op jit(solution)/shard_map/emit/pallas_call | solution.py:491

commit v5 on v3

--- a/solution.py
+++ b/solution.py
@@ -51,7 +51,7 @@
     slots_f, slots_c, send_f, send_c, recv_f, recv_c,
     field, alpha, bx, by, bz, rhs, near, edge_y, edge_x, diag, inverse_ref, scaled, total, resid,
     pack, face_y, halo_x, halo_y, rim_pack, rim_face, rim_x, rim_y, beta_pack,
-    sent_z, got_z, sent_y, got_y, sent_x, got_x, sent_yz, got_yz, sent_q, got_xz, got_xy, held_ref,
+    sent_z, got_z, sent_y, got_y, sent_x, got_x, sent_yz, got_yz, sent_q, got_xz, got_xy, line_weight, line_fix, pack_weight, held_ref,
     load_sem, held_sem, pair_send, pair_recv, halo_send, halo_recv, rim_send, rim_recv, out_sem,
     both_send, both_recv,
 ):
@@ -111,43 +111,44 @@
 
     def halo_copies(k):
         return [
+            copy_to(pack.at[k], halo_x.at[k, 1], halo_send.at[k, 0], halo_recv.at[k, 0], x_low),
+            copy_to(pack.at[k], halo_x.at[k, 0], halo_send.at[k, 1], halo_recv.at[k, 1], x_high),
+            copy_to(face_y.at[k, 0], halo_y.at[k, 1], halo_send.at[k, 2], halo_recv.at[k, 2], y_low),
+            copy_to(face_y.at[k, 1], halo_y.at[k, 0], halo_send.at[k, 3], halo_recv.at[k, 3], y_high),
             copy_to(field.at[k, 1], field.at[k, NZ + 1], halo_send.at[k, 4], halo_recv.at[k, 4], z_low),
             copy_to(field.at[k, NZ], field.at[k, 0], halo_send.at[k, 5], halo_recv.at[k, 5], z_high),
-            copy_to(face_y.at[k, 0], halo_y.at[k, 1], halo_send.at[k, 2], halo_recv.at[k, 2], y_low),
-            copy_to(face_y.at[k, 1], halo_y.at[k, 0], halo_send.at[k, 3], halo_recv.at[k, 3], y_high),
-            copy_to(pack.at[k], halo_x.at[k, 1], halo_send.at[k, 0], halo_recv.at[k, 0], x_low),
-            copy_to(pack.at[k], halo_x.at[k, 0], halo_send.at[k, 1], halo_recv.at[k, 1], x_high),
         ]
 
     first_halos = halo_copies(0)
 
+    def numbered(r, first, moves):
+        return [
+            copy_to(source, target, both_send.at[r, first + i], both_recv.at[r, first + i], device)
+            for i, (source, target, device) in enumerate(moves)
+        ]
+
     def edge_copies(r):
-        copies = []
+        moves = []
         for a in range(2):
             for b in range(2):
-                copies.append((sent_q.at[r], got_xy.at[r, 1 - a, 1 - b], {**x_sides[a], **y_sides[b]}))
+                device = {**x_sides[a], **y_sides[b]}
+                line = pl.ds(b * (ROWS - 1), 1)
+                moves.append((sent_q.at[r, pl.ds(0, 2), line], got_xy.at[r, 1 - a, 1 - b, pl.ds(0, 2), line], device))
         for a in range(2):
             for b in range(2):
-                copies.append((sent_q.at[r], got_xz.at[r, 1 - a, 1 - b], {**x_sides[a], **z_sides[b]}))
+                device = {**x_sides[a], **z_sides[b]}
+                moves.append((sent_q.at[r, 2], got_xz.at[r, 1 - a, 1 - b], device))
         for a in range(2):
             for b in range(2):
-                copies.append((sent_yz.at[r, a, b], got_yz.at[r, 1 - a, 1 - b], {**z_sides[a], **y_sides[b]}))
-        return [copy_to(m[0], m[1], both_send.at[r, i], both_recv.at[r, i], m[2]) for i, m in enumerate(copies)]
-
-    def face_copies(r):
-        count = 3 - r
-        copies = [
-            (sent_x.at[r, pl.ds(0, count)], got_x.at[r, 1 - a, pl.ds(0, count)], x_sides[a]) for a in range(2)
-        ]
-        copies += [
-            (sent_y.at[r, a, pl.ds(0, count)], got_y.at[r, 1 - a, pl.ds(0, count)], y_sides[a]) for a in range(2)
-        ]
-        copies += [
-            (sent_z.at[r, a, pl.ds(0, count)], got_z.at[r, 1 - a, pl.ds(0, count)], z_sides[a]) for a in range(2)
-        ]
-        return [
-            copy_to(m[0], m[1], both_send.at[r, 12 + i], both_recv.at[r, 12 + i], m[2]) for i, m in enumerate(copies)
-        ]
+                moves.append((sent_yz.at[r, a, b], got_yz.at[r, 1 - a, 1 - b], {**z_sides[a], **y_sides[b]}))
+        return numbered(r, 12, moves)
+
+    def face_copies(r, first, part):
+        moves = [(sent_x.at[r, part], got_x.at[r, 1 - a, part], x_sides[a]) for a in range(2)]
+        moves += [(sent_y.at[r, a, part], got_y.at[r, 1 - a, part], y_sides[a]) for a in range(2)]
+        moves += [(sent_z.at[r, a, part], got_z.at[r, 1 - a, part], z_sides[a]) for a in range(2)]
+        return numbered(r, first, moves)
+
     rims = [
         copy_to(rim_pack, rim_x, rim_send.at[0], rim_recv.at[0], x_low),
         copy_to(rim_face, rim_y, rim_send.at[1], rim_recv.at[1], y_low),
@@ -315,8 +316,8 @@
     for g, rows in enumerate(group_rows):
         z_pack = packed(0, g, bz[0, rows, :LANES], bz[0, rows, LANES:], z_pack)
         z_pack = packed(NZ - 1, g, bz[NZ, rows, :LANES], bz[NZ, rows, LANES:], z_pack)
-    beta_pack[0] = jnp.where(odd, rim_pack[...], pltpu.roll(rim_values, LANES - 1, 1))
-    beta_pack[1] = jnp.where(low_rim | high_rim, y_pack, 0.0)
+    beta_pack[0] = jnp.where(low_rim | high_rim, y_pack, 0.0)
+    beta_pack[1] = jnp.where(odd, rim_pack[...], pltpu.roll(rim_values, LANES - 1, 1))
     beta_pack[2] = z_pack
     sent_z[0, 0, 2] = inverse_ref[0]
     sent_z[0, 1, 2] = inverse_ref[NZ - 1]
@@ -381,6 +382,10 @@
                     value = value + near[4, z, rows, part] * halo_z_of(k, 0)[rows, part]
                 if last:
                     value = value + near[5, z, rows, part] * halo_z_of(k, 1)[rows, part]
+                for b in range(2):
+                    if k and k % 2 == 0 and (first or last) and g == b * (GROUPS - 1):
+                        line = jnp.broadcast_to(line_fix[0 if first else 1, b, :, part], (ROWS, LANES))
+                        value = value + jnp.where(row8 == b * (ROWS - 1), line, 0.0)
                 if k == SWEEPS:
                     resid[z, rows, part] = diag[z, rows, part] * value
                     continue
@@ -411,74 +416,86 @@
         carry = planes(lambda z, carry: inner(k, z, False, False, carry), carry, 1, NZ - 1)
         return inner(k, NZ - 1, False, True, carry)
 
-    def run_outer(k, x_halo):
-        sides = edge_x[...] * swapped(x_halo)
+    def run_outer(k, x_halo, extra=0.0):
+        sides = edge_x[...] * swapped(x_halo) + extra
         carry = outer(k, 0, True, False, sides, zero_pack)
         carry = planes(lambda z, carry: outer(k, z, False, False, sides, carry), carry, 1, NZ - 1)
         return outer(k, NZ - 1, False, True, sides, carry)
 
-    def spread_low(source, spot):
-        return pltpu.roll(source, (LANES - 2 * spot) % LANES, 1)
-
-    def spread_high(source, spot):
-        return pltpu.roll(source, 126 - 2 * spot, 1)
-
-    def ahead_z(r, k, side):
-        own = side * (NZ - 1)
-        sender = NZ - 1 - own
-        for j, part in enumerate(halves):
-            value = bz[side * NZ, :, part] * field[k, own + 1, :, part]
-            for b, at in ((0, 0), (1, NY - 1)):
-                line = jnp.broadcast_to(got_yz[r, side, b, 0, :, part], (NY, LANES))
-                value = value + jnp.where(row == at, line, 0.0)
-            source = got_xz[r, j, side, 0]
-            move = (spread_low, spread_high)[j]
-            column = jnp.concatenate([move(source, sender * GROUPS + g) for g in range(GROUPS)], axis=0)
-            value = value + jnp.where((first_lane, last_lane)[j], column, 0.0)
-            value = got_z[r, side, 1, :, part] + SECOND[k] * got_z[0, side, 2, :, part] * value
-            field[k + 1, side * (NZ + 1), :, part] = value
-
-    def ahead_y(r, k, side):
-        sender_group = (GROUPS - 1) * (1 - side)
-        sender_row = (ROWS - 1) * (1 - side)
-        face = (rim_face, rim_y)[side]
-        sources = [got_xy[r, j, side, 0] for j in range(2)]
-        for z in range(NZ):
-            for j, part in enumerate(halves):
-                value = face[z, :, part] * sent_y[r, side, 0, z, :, part]
-                if z == 0:
-                    value = value + got_yz[r, 0, side, 1, :, part]
-                if z == NZ - 1:
-                    value = value + got_yz[r, 1, side, 1, :, part]
-                column = (spread_low, spread_high)[j](sources[j], z * GROUPS + sender_group)
-                column = jnp.where(lane8 == (0, LANES - 1)[j], column, 0.0)
-                value = value + column[sender_row : sender_row + 1]
-                value = got_y[r, side, 1, z, :, part] + SECOND[k] * got_y[0, side, 2, z, :, part] * value
-                halo_y[k + 1, side, z, :, part] = value
-
     def either(ref_low, ref_high):
         return jnp.where(odd, ref_high, ref_low)
 
-    def ahead_x(r, k):
-        value = swapped(sent_q[r, 0])
-        below = either(got_xy[r, 0, 0, 1], got_xy[r, 1, 0, 1])
-        above = either(got_xy[r, 0, 1, 1], got_xy[r, 1, 1, 1])
-        shift = 2 * (GROUPS - 1)
-        value = value + jnp.where(low_rim, pltpu.roll(pltpu.roll(below, 1, 0), LANES - shift, 1), 0.0)
-        value = value + jnp.where(high_rim, pltpu.roll(pltpu.roll(above, ROWS - 1, 0), shift, 1), 0.0)
-        below = either(got_xz[r, 0, 0, 2], got_xz[r, 1, 0, 2])
-        above = either(got_xz[r, 0, 1, 2], got_xz[r, 1, 1, 2])
-        shift = 2 * GROUPS * (NZ - 1)
-        value = value + jnp.where(low_spots, pltpu.roll(below, LANES - shift, 1), 0.0)
-        value = value + jnp.where(high_spots, pltpu.roll(above, shift, 1), 0.0)
-        partial = either(got_x[r, 0, 1], got_x[r, 1, 1])
-        return partial + SECOND[k] * either(got_x[0, 0, 2], got_x[0, 1, 2]) * value
+    def ahead(r, k):
+        for side in range(2):
+            own = side * (NZ - 1)
+            for part in halves:
+                value = got_z[0, side, 2, :, part] * (bz[side * NZ, :, part] * field[k, own + 1, :, part])
+                field[k + 1, side * (NZ + 1), :, part] = got_z[r, side, 1, :, part] + SECOND[k] * value
+            face = (rim_face, rim_y)[side]
+            value = got_y[0, side, 2] * (face[...] * sent_y[r, side, 0])
+            halo_y[k + 1, side] = got_y[r, side, 1] + SECOND[k] * value
+        value = either(got_x[0, 0, 2], got_x[0, 1, 2]) * swapped(sent_q[r, 1])
+        return either(got_x[r, 0, 1], got_x[r, 1, 1]) + SECOND[k] * value
+
+    def weigh_edges():
+        y_pack = zero_pack
+        z_pack = zero_pack
+        for a in range(2):
+            z = a * (NZ - 1)
+            tiles = [near[4 + a, z, :, part] * got_z[0, a, 2, :, part] for part in halves]
+            for g, rows in enumerate(group_rows):
+                z_pack = packed(z, g, tiles[0][rows], tiles[1][rows], z_pack)
+            for b in range(2):
+                at = b * (NY - 1)
+                low = b * (ROWS - 1)
+                line_weight[a, b, 0] = near[4 + a, z, at : at + 1, :] * got_z[0, a, 2, at : at + 1, :]
+                line_weight[a, b, 1] = edge_y[b, z, low : low + 1, :] * got_y[0, b, 2, z]
+
+        def body(z, y_pack):
+            for b in range(2):
+                tiles = [
+                    edge_y[b, z, :, part] * jnp.broadcast_to(got_y[0, b, 2, z, :, part], (ROWS, LANES))
+                    for part in halves
+                ]
+                y_pack = packed(z, b * (GROUPS - 1), tiles[0], tiles[1], y_pack)
+            return y_pack
+
+        pack_weight[0] = edge_x[...] * swapped(either(got_x[0, 0, 2], got_x[0, 1, 2]))
+        pack_weight[1] = planes(body, y_pack)
+        pack_weight[2] = z_pack
+
+    def edge_fix(r, k):
+        for a in range(2):
+            for b in range(2):
+                value = line_weight[a, b, 0] * got_yz[r, a, b, 0] + line_weight[a, b, 1] * got_yz[r, a, b, 1]
+                line_fix[a, b] = SECOND[k] * value
+
+        def from_y(i):
+            below = swapped(either(got_xy[r, 0, 0, i], got_xy[r, 1, 0, i]))
+            above = swapped(either(got_xy[r, 0, 1, i], got_xy[r, 1, 1, i]))
+            shift = 2 * (GROUPS - 1)
+            below = jnp.where(low_rim, pltpu.roll(pltpu.roll(below, 1, 0), LANES - shift, 1), 0.0)
+            return below + jnp.where(high_rim, pltpu.roll(pltpu.roll(above, ROWS - 1, 0), shift, 1), 0.0)
+
+        def from_z(i):
+            below = swapped(either(got_xz[r, 0, 0], got_xz[r, 1, 0]))
+            above = swapped(either(got_xz[r, 0, 1], got_xz[r, 1, 1]))
+            shift = 2 * GROUPS * (NZ - 1)
+            back = (1 - i) * ROWS
+            below = jnp.where(low_spots, pltpu.roll(below, LANES - shift - back, 1), 0.0)
+            return below + jnp.where(high_spots, pltpu.roll(above, shift - back, 1), 0.0)
+
+        value = pack_weight[0] * (from_y(0) + from_z(1))
+        return SECOND[k] * (value + pack_weight[1] * from_y(1) + pack_weight[2] * from_z(0))
 
     def apply_two(r):
         k = 2 * r + 1
         own = sent_x[r, 0]
-        for i in range(3):
-            sent_q[r, i] = beta_pack[i] * own
+        sent_q[r, 0] = beta_pack[0] * own
+        across = beta_pack[1] * own
+        sent_q[r, 1] = across
+        ends = pltpu.roll(jnp.where(low_spots | high_spots, across, 0.0), ROWS, 1)
+        sent_q[r, 2] = beta_pack[2] * own + ends
         for a in range(2):
             z = a * (NZ - 1)
             for b in range(2):
@@ -486,14 +503,18 @@
                 at = b * (NY - 1)
                 sent_yz[r, a, b, 0] = (rim_face, rim_y)[b][z] * line
                 sent_yz[r, a, b, 1] = bz[a * NZ, at : at + 1, :] * line
-        copies = edge_copies(r)
-        for copy in copies:
+        far_copies = edge_copies(r)
+        for copy in far_copies:
             copy.start()
+
         sent_x[r, 1] = SECOND[k] * run_inner(k) + FIRST[k] * own
-        more = face_copies(r)
-        for copy in more:
+        near_copies = face_copies(r, 0, pl.ds(0, 2))
+        for copy in near_copies:
             copy.start()
-
+        if r == 0:
+            near_copies += face_copies(r, 6, pl.ds(2, 1))
+            for copy in near_copies[6:]:
+                copy.start()
         def sum_body(z, carry):
             for part in halves:
                 if r == 0:
@@ -505,17 +526,20 @@
             return carry
 
         planes(sum_body)
-        for copy in copies + more:
+        for copy in near_copies[:6]:
             copy.wait_recv()
         run_outer(k, either(got_x[r, 0, 0], got_x[r, 1, 0]))
         if k == SWEEPS - 1:
             x_out.start()
-        x_halo = ahead_x(r, k)
-        for side in range(2):
-            ahead_z(r, k, side)
-            ahead_y(r, k, side)
+        for copy in near_copies[6:]:
+            copy.wait_recv()
+        x_halo = ahead(r, k)
+        if r == 0:
+            weigh_edges()
         run_inner(k + 1)
-        return copies + more, run_outer(k + 1, x_halo)
+        for copy in far_copies:
+            copy.wait_recv()
+        return near_copies + far_copies, run_outer(k + 1, x_halo, edge_fix(r, k))
 
     x_out = pltpu.make_async_copy(total, x_hbm, out_sem.at[0])
     run_inner(0)
@@ -595,8 +619,11 @@
             pltpu.VMEM((2, 2, 2, 2, 1, NX), F32),
             pltpu.VMEM((2, 2, 2, 2, 1, NX), F32),
             pltpu.VMEM((2, 3, ROWS, LANES), F32),
-            pltpu.VMEM((2, 2, 2, 3, ROWS, LANES), F32),
-            pltpu.VMEM((2, 2, 2, 3, ROWS, LANES), F32),
+            pltpu.VMEM((2, 2, 2, ROWS, LANES), F32),
+            pltpu.VMEM((2, 2, 2, 2, ROWS, LANES), F32),
+            pltpu.VMEM((2, 2, 2, 1, NX), F32),
+            pltpu.VMEM((2, 2, 1, NX), F32),
+            pltpu.VMEM((3, ROWS, LANES), F32),
             pltpu.SMEM((1, 1, slots), jnp.int32),
             dma((6,)),
             dma((1,)),
@@ -607,8 +634,8 @@
             dma((3,)),
             dma((3,)),
             dma((2,)),
-            dma((2, 18)),
-            dma((2, 18)),
+            dma((2, 24)),
+            dma((2, 24)),
         ],
         compiler_params=pltpu.CompilerParams(
             collective_id=0, has_side_effects=True, vmem_limit_bytes=55767040

time: 34 us -> 31.9 us (0.938)
  Pallas kernels: 33.3 us -> 31.2 us
    pallas_call x1, Pallas kernels: 32.4 us -> 30.3 us  [local(): pl.pallas_call(kernel, out_shape=(jax.ShapeDtypeStruct(brick, F32), jax.S...]
where the time goes in v5:
time: 31.9 us; the launch traced here: 31.8 us
  Pallas kernels  31.2 us (98%)
  between operations  0.64 us (2%)
    pallas_call x1, Pallas kernels, local(): pl.pallas_call(kernel, out_shape=(jax.ShapeDtypeStruct(brick, F32), jax.S...  30.3 us
    pallas_call x1, Pallas kernels, local(): pl.pallas_call(emit, out_shape=(jax.ShapeDtypeStruct(brick, F32), jax.Sha...  0.89 us

profile of v5, /device:TPU:1, one launch (start us, length us, event | category | flops | bytes accessed | tf_op | source)
XLA Modules:
  0.0 31.8 jit_solution(11055884347544835139)
XLA Ops:
  0.6 30.3 %smooth.1 = (f32[16,24,256]{2,1,0:T(8,128)S(1)}, f32[16,24,256]{2,1,0:T(8,128)S(1)}) custom-call(f32[2,2,16,2,8,256]{5,4,3,2,1,0:T(8,128)} %bitcast.3, bf16[4,2,16,2,8,256]{5,4,3,2,1,0:T(8,128)(2,1)} %bitcast.4, s32[1,1,2]{2,1,0:T(1,128)} %bitcast.5), custom_call_target="tpu_custom_call" | custom-call | tf_op jit(solution)/shard_map/smooth/pallas_call | solution.py:578
  30.9 0.9 %emit.1 = (f32[16,24,256]{2,1,0:T(8,128)}, f32[16,24,256]{2,1,0:T(8,128)}) custom-call(f32[16,24,256]{2,1,0:T(8,128)S(1)} %get-tuple-element.4.x_ref, f32[16,24,256]{2,1,0:T(8,128)S(1)} %get-tuple-element.5.r_ref), custom_call_target="tpu_custom_call" | custom-call | tf_op jit(solution)/shard_map/emit/pallas_call | solution.py:645

commit v6 on v5

--- a/solution.py
+++ b/solution.py
@@ -66,10 +66,7 @@
     barrier = pltpu.get_barrier_semaphore()
     x_sides, y_sides, z_sides = (x_low, x_high), (y_low, y_high), (z_low, z_high)
     faces = [x_low, x_high, y_low, y_high, z_low, z_high]
-    edges = [{**a, **b} for a in z_sides for b in y_sides]
-    edges += [{**a, **b} for a in x_sides for b in z_sides]
-    edges += [{**a, **b} for a in x_sides for b in y_sides]
-    for neighbour in faces + edges:
+    for neighbour in faces:
         pl.semaphore_signal(barrier, inc=1, device_id=neighbour, device_id_type=MESH)
 
     load_held = pltpu.make_async_copy(held_hbm, held_ref, held_sem.at[0])
@@ -181,7 +178,7 @@
 
     loads_f[0].wait()
     prepare(slots_f.at[0], send_f.at[0])
-    pl.semaphore_wait(barrier, len(faces) + len(edges))
+    pl.semaphore_wait(barrier, len(faces))
     pair_f[0].start()
     for c in (1, 2, 3, 0):
         loads_c[c].wait()

time: 31.9 us -> 29.9 us (0.937)
  Pallas kernels: 31.2 us -> 29.1 us
    pallas_call x1, Pallas kernels: 30.3 us -> 28.2 us  [local(): pl.pallas_call(kernel, out_shape=(jax.ShapeDtypeStruct(brick, F32), jax.S...]
where the time goes in v6:
time: 29.9 us; the launch traced here: 29.8 us
  Pallas kernels  29.1 us (97%)
  between operations  0.64 us (2%)
    pallas_call x1, Pallas kernels, local(): pl.pallas_call(kernel, out_shape=(jax.ShapeDtypeStruct(brick, F32), jax.S...  28.2 us
    pallas_call x1, Pallas kernels, local(): pl.pallas_call(emit, out_shape=(jax.ShapeDtypeStruct(brick, F32), jax.Sha...  0.89 us

profile of v6, /device:TPU:1, one launch (start us, length us, event | category | flops | bytes accessed | tf_op | source)
XLA Modules:
  0.0 29.8 jit_solution(4536045859691134626)
XLA Ops:
  0.6 28.2 %smooth.1 = (f32[16,24,256]{2,1,0:T(8,128)S(1)}, f32[16,24,256]{2,1,0:T(8,128)S(1)}) custom-call(f32[2,2,16,2,8,256]{5,4,3,2,1,0:T(8,128)} %bitcast.3, bf16[4,2,16,2,8,256]{5,4,3,2,1,0:T(8,128)(2,1)} %bitcast.4, s32[1,1,2]{2,1,0:T(1,128)} %bitcast.5), custom_call_target="tpu_custom_call" | custom-call | tf_op jit(solution)/shard_map/smooth/pallas_call | solution.py:575
  28.9 0.9 %emit.1 = (f32[16,24,256]{2,1,0:T(8,128)}, f32[16,24,256]{2,1,0:T(8,128)}) custom-call(f32[16,24,256]{2,1,0:T(8,128)S(1)} %get-tuple-element.4.x_ref, f32[16,24,256]{2,1,0:T(8,128)S(1)} %get-tuple-element.5.r_ref), custom_call_target="tpu_custom_call" | custom-call | tf_op jit(solution)/shard_map/emit/pallas_call | solution.py:642

commit v7 on v6

--- a/solution.py
+++ b/solution.py
@@ -51,9 +51,10 @@
     slots_f, slots_c, send_f, send_c, recv_f, recv_c,
     field, alpha, bx, by, bz, rhs, near, edge_y, edge_x, diag, inverse_ref, scaled, total, resid,
     pack, face_y, halo_x, halo_y, rim_pack, rim_face, rim_x, rim_y, beta_pack,
-    sent_z, got_z, sent_y, got_y, sent_x, got_x, sent_yz, got_yz, sent_q, got_xz, got_xy, line_weight, line_fix, pack_weight, held_ref,
+    sent_z, got_z, sent_y, got_y, sent_x, got_x, sent_yz, got_yz, sent_q, got_xz, got_xy, line_weight, line_fix, pack_weight,
+    part_x, part_y, part_z, give_x, give_y, give_z, face_z, held_ref,
     load_sem, held_sem, pair_send, pair_recv, halo_send, halo_recv, rim_send, rim_recv, out_sem,
-    both_send, both_recv,
+    both_send, both_recv, part_send, part_recv,
 ):
     group = lax.axis_index("gy")
     half = lax.rem(group, 2)
@@ -112,8 +113,8 @@
             copy_to(pack.at[k], halo_x.at[k, 0], halo_send.at[k, 1], halo_recv.at[k, 1], x_high),
             copy_to(face_y.at[k, 0], halo_y.at[k, 1], halo_send.at[k, 2], halo_recv.at[k, 2], y_low),
             copy_to(face_y.at[k, 1], halo_y.at[k, 0], halo_send.at[k, 3], halo_recv.at[k, 3], y_high),
-            copy_to(field.at[k, 1], field.at[k, NZ + 1], halo_send.at[k, 4], halo_recv.at[k, 4], z_low),
-            copy_to(field.at[k, NZ], field.at[k, 0], halo_send.at[k, 5], halo_recv.at[k, 5], z_high),
+            copy_to(face_z.at[0], field.at[k, NZ + 1], halo_send.at[k, 4], halo_recv.at[k, 4], z_low),
+            copy_to(face_z.at[1], field.at[k, 0], halo_send.at[k, 5], halo_recv.at[k, 5], z_high),
         ]
 
     first_halos = halo_copies(0)
@@ -149,7 +150,7 @@
     rims = [
         copy_to(rim_pack, rim_x, rim_send.at[0], rim_recv.at[0], x_low),
         copy_to(rim_face, rim_y, rim_send.at[1], rim_recv.at[1], y_low),
-        copy_to(bz.at[0], bz.at[NZ], rim_send.at[2], rim_recv.at[2], z_low),
+        copy_to(face_z.at[2], bz.at[NZ], rim_send.at[2], rim_recv.at[2], z_low),
     ]
 
     def planes(body, carry=0, first=0, last=NZ):
@@ -171,79 +172,111 @@
         ).astype(F32)
 
     def packed(z, g, tile_low, tile_high, carry):
-        spot = z * GROUPS + g
+        return packed_at(z * GROUPS + g, tile_low, tile_high, carry)
+
+    def packed_at(spot, tile_low, tile_high, carry):
         both = jnp.where(lane8 == 0, tile_low, tile_high)
         moved = pltpu.roll(both, 2 * spot + 1, 1)
         return jnp.where(spots == spot, moved, carry)
 
+    region = [first_slab + g // 2 for g in range(2 * GROUPS)]
+
+    def chosen(slab, first, second):
+        zero = jnp.zeros(first.shape, first.dtype)
+        return lax.select(id0 == slab, first, lax.select(id1 == slab, second, zero)).astype(F32)
+
+    def part_columns(slots, index):
+        def body(z, carry):
+            for h in range(2):
+                value = carry[h]
+                for g in range(GROUPS):
+                    at = GROUPS * h + g
+                    tile = chosen(region[at], slots[0, z, at % 2], slots[1, z, at % 2])
+                    value = packed(z, g, tile[:, :LANES], tile[:, LANES:], value)
+                carry = (value, carry[1]) if h == 0 else (carry[0], value)
+            return carry
+
+        part_x[0, index], part_x[1, index] = planes(body, (zero_pack, zero_pack))
+
+    def part_planes(slots, z, index):
+        for at in range(2 * GROUPS):
+            rows = slice((at % GROUPS) * ROWS, (at % GROUPS + 1) * ROWS)
+            part_z[at // GROUPS, index, rows, :] = chosen(region[at], slots[0, z, at % 2], slots[1, z, at % 2])
+
+    def part_rows(slots, side, index):
+        def body(z, carry):
+            for h in range(2):
+                at = GROUPS * h + side * (GROUPS - 1)
+                line = slice(side * (ROWS - 1), side * (ROWS - 1) + 1)
+                part_y[h, index, z] = chosen(region[at], slots[0, z, at % 2, line], slots[1, z, at % 2, line])
+            return carry
+
+        planes(body)
+
+    gives = [
+        copy_to(part_x.at[1 - half], give_x, part_send.at[0], part_recv.at[0], partner),
+        copy_to(part_y.at[1 - half], give_y, part_send.at[1], part_recv.at[1], partner),
+        copy_to(part_z.at[1 - half], give_z, part_send.at[2], part_recv.at[2], partner),
+    ]
+    zero_pack = jnp.zeros((ROWS, LANES), F32)
+
+    def plain(slots, received, out, shift=0):
+        def body(z, carry):
+            for g in range(GROUPS):
+                out[z + shift, g * ROWS : (g + 1) * ROWS, :] = assembled(slots, received, z, g)
+            return carry
+
+        planes(body)
+
     loads_f[0].wait()
+    part_columns(slots_f.at[0], 0)
+    part_planes(slots_f.at[0], 0, 0)
+    part_planes(slots_f.at[0], NZ - 1, 1)
+    part_rows(slots_f.at[0], 0, 0)
+    part_rows(slots_f.at[0], 1, 1)
+    loads_c[1].wait()
+    part_columns(slots_c.at[1], 1)
+    loads_c[2].wait()
+    part_rows(slots_c.at[2], 0, 2)
+    loads_c[3].wait()
+    part_planes(slots_c.at[3], 0, 2)
+    pl.semaphore_wait(barrier, len(faces))
+    for copy in gives:
+        copy.start()
+    gives[0].wait_recv()
+    pack[0] = part_x[half, 0] + give_x[0]
+    rim_pack[...] = part_x[half, 1] + give_x[1]
+    first_halos[0].start()
+    first_halos[1].start()
+    rims[0].start()
+    gives[1].wait_recv()
+    for b in range(2):
+        face_y[0, b] = part_y[half, b] + give_y[b]
+    rim_face[...] = part_y[half, 2] + give_y[2]
+    first_halos[2].start()
+    first_halos[3].start()
+    rims[1].start()
+    gives[2].wait_recv()
+    for i in range(3):
+        face_z[i] = part_z[half, i] + give_z[i]
+    rims[2].start()
+    first_halos[4].start()
+    first_halos[5].start()
     prepare(slots_f.at[0], send_f.at[0])
-    pl.semaphore_wait(barrier, len(faces))
     pair_f[0].start()
     for c in (1, 2, 3, 0):
-        loads_c[c].wait()
+        if c == 0:
+            loads_c[c].wait()
         prepare(slots_c.at[c], send_c.at[c])
         pair_c[c].start()
     loads_f[1].wait()
     prepare(slots_f.at[1], send_f.at[1])
     pair_f[1].start()
-
-    zero_pack = jnp.zeros((ROWS, LANES), F32)
-
     pair_f[0].wait_recv()
-
-    def start_body(z, carry):
-        for g in range(GROUPS):
-            value = assembled(slots_f.at[0], recv_f.at[0], z, g)
-            field[0, z + 1, g * ROWS : (g + 1) * ROWS, :] = value
-            if g == 0:
-                face_y[0, 0, z] = value[0:1, :]
-            if g == GROUPS - 1:
-                face_y[0, 1, z] = value[ROWS - 1 : ROWS, :]
-            carry = packed(z, g, value[:, :LANES], value[:, LANES:], carry)
-        return carry
-
-    pack[0] = planes(start_body, zero_pack)
-    for copy in first_halos:
-        copy.start()
-
-    pair_c[1].wait_recv()
-
-    def bx_body(z, carry):
-        for g in range(GROUPS):
-            value = assembled(slots_c.at[1], recv_c.at[1], z, g)
-            bx[z, g * ROWS : (g + 1) * ROWS, :] = value
-            carry = packed(z, g, value[:, :LANES], value[:, LANES:], carry)
-        return carry
-
-    rim_pack[...] = planes(bx_body, zero_pack)
-    rims[0].start()
-    pair_c[2].wait_recv()
-
-    def by_body(z, carry):
-        for g in range(GROUPS):
-            value = assembled(slots_c.at[2], recv_c.at[2], z, g)
-            by[z, g * ROWS : (g + 1) * ROWS, :] = value
-            if g == 0:
-                rim_face[z] = value[0:1, :]
-        return carry
-
-    planes(by_body)
-    rims[1].start()
-
-    def plain(slots, received, out):
-        def body(z, carry):
-            for g in range(GROUPS):
-                out[z, g * ROWS : (g + 1) * ROWS, :] = assembled(slots, received, z, g)
-            return carry
-
-        planes(body)
-
-    pair_c[3].wait_recv()
-    plain(slots_c.at[3], recv_c.at[3], bz)
-    rims[2].start()
-    pair_c[0].wait_recv()
-    plain(slots_c.at[0], recv_c.at[0], alpha)
+    plain(slots_f.at[0], recv_f.at[0], field.at[0], 1)
+    for c, out in ((1, bx), (2, by), (3, bz), (0, alpha)):
+        pair_c[c].wait_recv()
+        plain(slots_c.at[c], recv_c.at[c], out)
     pair_f[1].wait_recv()
     plain(slots_f.at[1], recv_f.at[1], rhs)
     for copy in rims:
@@ -500,18 +533,18 @@
                 at = b * (NY - 1)
                 sent_yz[r, a, b, 0] = (rim_face, rim_y)[b][z] * line
                 sent_yz[r, a, b, 1] = bz[a * NZ, at : at + 1, :] * line
+        near_copies = face_copies(r, 0, pl.ds(0, 1))
         far_copies = edge_copies(r)
-        for copy in far_copies:
+        for copy in far_copies[:8] + near_copies + far_copies[8:]:
             copy.start()
 
         sent_x[r, 1] = SECOND[k] * run_inner(k) + FIRST[k] * own
-        near_copies = face_copies(r, 0, pl.ds(0, 2))
-        for copy in near_copies:
+        ahead_copies = face_copies(r, 24, pl.ds(1, 1))
+        if r == 0:
+            ahead_copies += face_copies(r, 6, pl.ds(2, 1))
+        for copy in ahead_copies:
             copy.start()
-        if r == 0:
-            near_copies += face_copies(r, 6, pl.ds(2, 1))
-            for copy in near_copies[6:]:
-                copy.start()
+
         def sum_body(z, carry):
             for part in halves:
                 if r == 0:
@@ -523,12 +556,12 @@
             return carry
 
         planes(sum_body)
-        for copy in near_copies[:6]:
+        for copy in near_copies:
             copy.wait_recv()
         run_outer(k, either(got_x[r, 0, 0], got_x[r, 1, 0]))
         if k == SWEEPS - 1:
             x_out.start()
-        for copy in near_copies[6:]:
+        for copy in ahead_copies:
             copy.wait_recv()
         x_halo = ahead(r, k)
         if r == 0:
@@ -536,7 +569,7 @@
         run_inner(k + 1)
         for copy in far_copies:
             copy.wait_recv()
-        return near_copies + far_copies, run_outer(k + 1, x_halo, edge_fix(r, k))
+        return near_copies + far_copies + ahead_copies, run_outer(k + 1, x_halo, edge_fix(r, k))
 
     x_out = pltpu.make_async_copy(total, x_hbm, out_sem.at[0])
     run_inner(0)
@@ -547,7 +580,7 @@
     second_copies, unused = apply_two(1)
     r_out = pltpu.make_async_copy(resid, r_hbm, out_sem.at[1])
     r_out.start()
-    for copy in pair_f + pair_c + rims + first_halos + first_copies + second_copies:
+    for copy in gives + pair_f + pair_c + rims + first_halos + first_copies + second_copies:
         copy.wait_send()
     x_out.wait()
     r_out.wait()
@@ -621,6 +654,13 @@
             pltpu.VMEM((2, 2, 2, 1, NX), F32),
             pltpu.VMEM((2, 2, 1, NX), F32),
             pltpu.VMEM((3, ROWS, LANES), F32),
+            pltpu.VMEM((2, 2, ROWS, LANES), F32),
+            pltpu.VMEM((2, 3, NZ, 1, NX), F32),
+            pltpu.VMEM((2, 3, NY, NX), F32),
+            pltpu.VMEM((2, ROWS, LANES), F32),
+            pltpu.VMEM((3, NZ, 1, NX), F32),
+            pltpu.VMEM((3, NY, NX), F32),
+            pltpu.VMEM((3, NY, NX), F32),
             pltpu.SMEM((1, 1, slots), jnp.int32),
             dma((6,)),
             dma((1,)),
@@ -631,8 +671,10 @@
             dma((3,)),
             dma((3,)),
             dma((2,)),
-            dma((2, 24)),
-            dma((2, 24)),
+            dma((2, 30)),
+            dma((2, 30)),
+            dma((3,)),
+            dma((3,)),
         ],
         compiler_params=pltpu.CompilerParams(
             collective_id=0, has_side_effects=True, vmem_limit_bytes=55767040

time: 29.9 us -> 29 us (0.970)
  Pallas kernels: 29.1 us -> 28.3 us
    pallas_call x1, Pallas kernels: 28.2 us -> 27.4 us  [local(): pl.pallas_call(kernel, out_shape=(jax.ShapeDtypeStruct(brick, F32), jax.S...]
where the time goes in v7:
time: 29 us; the launch traced here: 28.9 us
  Pallas kernels  28.3 us (98%)
  between operations  0.64 us (2%)
    pallas_call x1, Pallas kernels, local(): pl.pallas_call(kernel, out_shape=(jax.ShapeDtypeStruct(brick, F32), jax.S...  27.4 us
    pallas_call x1, Pallas kernels, local(): pl.pallas_call(emit, out_shape=(jax.ShapeDtypeStruct(brick, F32), jax.Sha...  0.89 us

profile of v7, /device:TPU:1, one launch (start us, length us, event | category | flops | bytes accessed | tf_op | source)
XLA Modules:
  0.0 28.9 jit_solution(2556154032290200828)
XLA Ops:
  0.6 27.4 %smooth.1 = (f32[16,24,256]{2,1,0:T(8,128)S(1)}, f32[16,24,256]{2,1,0:T(8,128)S(1)}) custom-call(f32[2,2,16,2,8,256]{5,4,3,2,1,0:T(8,128)} %bitcast.3, bf16[4,2,16,2,8,256]{5,4,3,2,1,0:T(8,128)(2,1)} %bitcast.4, s32[1,1,2]{2,1,0:T(1,128)} %bitcast.5), custom_call_target="tpu_custom_call" | custom-call | tf_op jit(solution)/shard_map/smooth/pallas_call | solution.py:608
  28.0 0.9 %emit.1 = (f32[16,24,256]{2,1,0:T(8,128)}, f32[16,24,256]{2,1,0:T(8,128)}) custom-call(f32[16,24,256]{2,1,0:T(8,128)S(1)} %get-tuple-element.4.x_ref, f32[16,24,256]{2,1,0:T(8,128)S(1)} %get-tuple-element.5.r_ref), custom_call_target="tpu_custom_call" | custom-call | tf_op jit(solution)/shard_map/emit/pallas_call | solution.py:684

commit v8 on v7

--- a/solution.py
+++ b/solution.py
@@ -279,63 +279,104 @@
         plain(slots_c.at[c], recv_c.at[c], out)
     pair_f[1].wait_recv()
     plain(slots_f.at[1], recv_f.at[1], rhs)
+    halves = (slice(0, LANES), slice(LANES, NX))
+    group_rows = [slice(g * ROWS, (g + 1) * ROWS) for g in range(GROUPS)]
+    def gather(z, last):
+        low_rolled = pltpu.roll(bx[z, :, :LANES], LANES - 1, 1)
+        high_rolled = pltpu.roll(bx[z, :, LANES:], LANES - 1, 1)
+        upper_x = (jnp.where(last_lane, high_rolled, low_rolled), jnp.where(last_lane, 0.0, high_rolled))
+        low, high = field[0, z + 1, :, :LANES], field[0, z + 1, :, LANES:]
+        low_after, high_after = pltpu.roll(low, LANES - 1, 1), pltpu.roll(high, LANES - 1, 1)
+        low_before, high_before = pltpu.roll(low, 1, 1), pltpu.roll(high, 1, 1)
+        x_before = (low_before, jnp.where(first_lane, low_before, high_before))
+        x_after = (jnp.where(last_lane, high_after, low_after), high_after)
+        for j, part in enumerate(halves):
+            here = (low, high)[j]
+            lower_x = bx[z, :, part]
+            here_y = by[z, :, part]
+            upper_y = jnp.where(end_row, 0.0, pltpu.roll(here_y, NY - 1, 0))
+            centre = alpha[z, :, part] + lower_x + upper_x[j] + here_y + upper_y + bz[z, :, part]
+            lower_x = jnp.where(first_lane, 0.0, lower_x) if j == 0 else lower_x
+            lower_y = jnp.where(row == 0, 0.0, here_y)
+            value = rhs[z, :, part] + lower_x * x_before[j] + upper_x[j] * x_after[j]
+            value = value + lower_y * pltpu.roll(here, 1, 0) + upper_y * pltpu.roll(here, NY - 1, 0)
+            if not isinstance(z, int) or z > 0:
+                value = value + bz[z, :, part] * field[0, z, :, part]
+            if not last:
+                centre = centre + bz[z + 1, :, part]
+                value = value + bz[z + 1, :, part] * field[0, z + 2, :, part]
+            near[0, z, :, part] = lower_x
+            near[1, z, :, part] = upper_x[j]
+            near[2, z, :, part] = lower_y
+            near[3, z, :, part] = upper_y
+            scaled[z, :, part] = value
+            diag[z, :, part] = centre
+
+    def gather_body(z, carry):
+        gather(z, False)
+        return carry
+
+    gather(0, False)
+    planes(gather_body, 0, 1, NZ - 1)
+    gather(NZ - 1, True)
     for copy in rims:
         copy.wait_recv()
-
-    halves = (slice(0, LANES), slice(LANES, NX))
-    group_rows = [slice(g * ROWS, (g + 1) * ROWS) for g in range(GROUPS)]
     rim_values = rim_x[...]
 
-    def scale_body(z, carry):
-        low_rolled = pltpu.roll(bx[z, :, :LANES], LANES - 1, 1)
-        high_rolled = pltpu.roll(bx[z, :, LANES:], LANES - 1, 1)
+    def scale(z, last, carry):
         edge = jnp.concatenate(
             [pltpu.roll(rim_values, 126 - 2 * (z * GROUPS + g), 1) for g in range(GROUPS)], axis=0
         )
-        upper_x = (jnp.where(last_lane, high_rolled, low_rolled), jnp.where(last_lane, edge, high_rolled))
-        before = []
-        after = []
+        edge = jnp.where(last_lane, edge, 0.0)
+        sides = []
         inverses = []
         uppers = []
         for j, part in enumerate(halves):
-            here_y = by[z, :, part]
-            upper_y = jnp.where(
-                end_row, jnp.broadcast_to(rim_y[z, :, part], (NY, LANES)), pltpu.roll(here_y, NY - 1, 0)
-            )
-            faces = [bx[z, :, part], upper_x[j], here_y, upper_y, bz[z, :, part], bz[z + 1, :, part]]
-            centre = alpha[z, :, part]
-            for face in faces:
-                centre = centre + face
+            rim_row = jnp.where(end_row, jnp.broadcast_to(rim_y[z, :, part], (NY, LANES)), 0.0)
+            centre = diag[z, :, part] + rim_row
+            if j == 1:
+                centre = centre + edge
+            if last:
+                centre = centre + bz[z + 1, :, part]
             inverse = 1.0 / centre
             inverses.append(inverse)
+            diag[z, :, part] = centre
             inverse_ref[z, :, part] = inverse
+            scaled[z, :, part] = inverse * scaled[z, :, part] - field[0, z + 1, :, part]
             sent_y[0, 0, 2, z, :, part] = inverse[:1]
             sent_y[0, 1, 2, z, :, part] = inverse[NY - 1 :]
-            uppers.append(upper_y[NY - ROWS :])
-            diag[z, :, part] = centre
-            scaled[z, :, part] = inverse * rhs[z, :, part]
-            weights = [inverse * face for face in faces]
-            before.append(weights[0])
-            after.append(weights[1])
-            if j == 0:
-                weights[0] = jnp.where(first_lane, 0.0, weights[0])
-            else:
-                weights[1] = jnp.where(last_lane, 0.0, weights[1])
-            edge_y[0, z, :, part] = jnp.where(row8 == 0, weights[2][:ROWS], 0.0)
-            edge_y[1, z, :, part] = jnp.where(row8 == ROWS - 1, weights[3][NY - ROWS :], 0.0)
-            weights[2] = jnp.where(row == 0, 0.0, weights[2])
-            weights[3] = jnp.where(end_row, 0.0, weights[3])
-            for i, weight in enumerate(weights):
-                near[i, z, :, part] = weight
+            uppers.append(rim_row[NY - ROWS :])
+            sides.append(inverse * (bx[z, :, part] if j == 0 else edge))
+            edge_y[0, z, :, part] = jnp.where(row8 == 0, inverse[:ROWS] * by[z, :ROWS, part], 0.0)
+            edge_y[1, z, :, part] = inverse[NY - ROWS :] * rim_row[NY - ROWS :]
+            if isinstance(z, int) and z == 0:
+                near[4, z, :, part] = inverse * bz[z, :, part]
+            if last:
+                near[5, z, :, part] = inverse * bz[z + 1, :, part]
         edge_pack, inverse_pack, y_pack = carry
         for g, rows in enumerate(group_rows):
-            edge_pack = packed(z, g, before[0][rows], after[1][rows], edge_pack)
+            edge_pack = packed(z, g, sides[0][rows], sides[1][rows], edge_pack)
             inverse_pack = packed(z, g, inverses[0][rows], inverses[1][rows], inverse_pack)
         y_pack = packed(z, 0, by[z, :ROWS, :LANES], by[z, :ROWS, LANES:], y_pack)
         y_pack = packed(z, GROUPS - 1, uppers[0], uppers[1], y_pack)
         return edge_pack, inverse_pack, y_pack
 
-    edge_x[...], sent_x[0, 2], y_pack = planes(scale_body, (zero_pack, zero_pack, zero_pack))
+    def weigh(z, first, last):
+        inverse = inverse_ref[z]
+        for i in range(4):
+            near[i, z] = inverse * near[i, z]
+        if not first:
+            near[4, z] = inverse * bz[z]
+        if not last:
+            near[5, z] = inverse * bz[z + 1]
+
+    def weigh_body(z, carry):
+        weigh(z, False, False)
+        return carry
+
+    carry = scale(0, False, (zero_pack, zero_pack, zero_pack))
+    carry = planes(lambda z, carry: scale(z, False, carry), carry, 1, NZ - 1)
+    edge_x[...], sent_x[0, 2], y_pack = scale(NZ - 1, True, carry)
     odd = lane8 - 2 * spots == 1
     spot_group = spots - GROUPS * (spots // GROUPS)
     low_rim = (spot_group == 0) & (row8 == 0)
@@ -538,6 +579,10 @@
         for copy in far_copies[:8] + near_copies + far_copies[8:]:
             copy.start()
 
+        if r == 0:
+            weigh(0, True, False)
+            planes(weigh_body, 0, 1, NZ - 1)
+            weigh(NZ - 1, False, True)
         sent_x[r, 1] = SECOND[k] * run_inner(k) + FIRST[k] * own
         ahead_copies = face_copies(r, 24, pl.ds(1, 1))
         if r == 0:
@@ -572,7 +617,6 @@
         return near_copies + far_copies + ahead_copies, run_outer(k + 1, x_halo, edge_fix(r, k))
 
     x_out = pltpu.make_async_copy(total, x_hbm, out_sem.at[0])
-    run_inner(0)
     for copy in first_halos:
         copy.wait_recv()
     sent_x[0, 0] = run_outer(0, either(halo_x[0, 0], halo_x[0, 1]))

time: 29 us -> 28.4 us (0.979)
  Pallas kernels: 28.3 us -> 27.7 us
    pallas_call x1, Pallas kernels: 27.4 us -> 26.8 us  [local(): pl.pallas_call(kernel, out_shape=(jax.ShapeDtypeStruct(brick, F32), jax.S...]
where the time goes in v8:
time: 28.4 us; the launch traced here: 28.3 us
  Pallas kernels  27.7 us (98%)
  between operations  0.64 us (2%)
    pallas_call x1, Pallas kernels, local(): pl.pallas_call(kernel, out_shape=(jax.ShapeDtypeStruct(brick, F32), jax.S...  26.8 us
    pallas_call x1, Pallas kernels, local(): pl.pallas_call(emit, out_shape=(jax.ShapeDtypeStruct(brick, F32), jax.Sha...  0.89 us

profile of v8, /device:TPU:1, one launch (start us, length us, event | category | flops | bytes accessed | tf_op | source)
XLA Modules:
  0.0 28.3 jit_solution(5979218000205789387)
XLA Ops:
  0.6 26.8 %smooth.1 = (f32[16,24,256]{2,1,0:T(8,128)S(1)}, f32[16,24,256]{2,1,0:T(8,128)S(1)}) custom-call(f32[2,2,16,2,8,256]{5,4,3,2,1,0:T(8,128)} %bitcast.3, bf16[4,2,16,2,8,256]{5,4,3,2,1,0:T(8,128)(2,1)} %bitcast.4, s32[1,1,2]{2,1,0:T(1,128)} %bitcast.5), custom_call_target="tpu_custom_call" | custom-call | tf_op jit(solution)/shard_map/smooth/pallas_call | solution.py:652
  27.4 0.9 %emit.1 = (f32[16,24,256]{2,1,0:T(8,128)}, f32[16,24,256]{2,1,0:T(8,128)}) custom-call(f32[16,24,256]{2,1,0:T(8,128)S(1)} %get-tuple-element.4.x_ref, f32[16,24,256]{2,1,0:T(8,128)S(1)} %get-tuple-element.5.r_ref), custom_call_target="tpu_custom_call" | custom-call | tf_op jit(solution)/shard_map/emit/pallas_call | solution.py:728

commit v9 on v8

--- a/solution.py
+++ b/solution.py
@@ -319,6 +319,7 @@
     gather(0, False)
     planes(gather_body, 0, 1, NZ - 1)
     gather(NZ - 1, True)
+    low_pack = planes(lambda z, carry: packed(z, 0, by[z, :ROWS, :LANES], by[z, :ROWS, LANES:], carry), zero_pack)
     for copy in rims:
         copy.wait_recv()
     rim_values = rim_x[...]
@@ -353,30 +354,27 @@
                 near[4, z, :, part] = inverse * bz[z, :, part]
             if last:
                 near[5, z, :, part] = inverse * bz[z + 1, :, part]
-        edge_pack, inverse_pack, y_pack = carry
+        edge_pack, y_pack = carry
         for g, rows in enumerate(group_rows):
             edge_pack = packed(z, g, sides[0][rows], sides[1][rows], edge_pack)
-            inverse_pack = packed(z, g, inverses[0][rows], inverses[1][rows], inverse_pack)
-        y_pack = packed(z, 0, by[z, :ROWS, :LANES], by[z, :ROWS, LANES:], y_pack)
         y_pack = packed(z, GROUPS - 1, uppers[0], uppers[1], y_pack)
-        return edge_pack, inverse_pack, y_pack
-
-    def weigh(z, first, last):
+        return edge_pack, y_pack
+
+    def weigh(z, first, last, carry):
         inverse = inverse_ref[z]
+        for g, rows in enumerate(group_rows):
+            carry = packed(z, g, inverse[rows, :LANES], inverse[rows, LANES:], carry)
         for i in range(4):
             near[i, z] = inverse * near[i, z]
         if not first:
             near[4, z] = inverse * bz[z]
         if not last:
             near[5, z] = inverse * bz[z + 1]
-
-    def weigh_body(z, carry):
-        weigh(z, False, False)
         return carry
 
-    carry = scale(0, False, (zero_pack, zero_pack, zero_pack))
+    carry = scale(0, False, (zero_pack, low_pack))
     carry = planes(lambda z, carry: scale(z, False, carry), carry, 1, NZ - 1)
-    edge_x[...], sent_x[0, 2], y_pack = scale(NZ - 1, True, carry)
+    edge_x[...], y_pack = scale(NZ - 1, True, carry)
     odd = lane8 - 2 * spots == 1
     spot_group = spots - GROUPS * (spots // GROUPS)
     low_rim = (spot_group == 0) & (row8 == 0)
@@ -580,9 +578,9 @@
             copy.start()
 
         if r == 0:
-            weigh(0, True, False)
-            planes(weigh_body, 0, 1, NZ - 1)
-            weigh(NZ - 1, False, True)
+            carry = weigh(0, True, False, zero_pack)
+            carry = planes(lambda z, carry: weigh(z, False, False, carry), carry, 1, NZ - 1)
+            sent_x[0, 2] = weigh(NZ - 1, False, True, carry)
         sent_x[r, 1] = SECOND[k] * run_inner(k) + FIRST[k] * own
         ahead_copies = face_copies(r, 24, pl.ds(1, 1))
         if r == 0:

time: 28.4 us -> 28.3 us (level)
  no operation moved by 1% of the time
where the time goes in v9:
time: 28.3 us; the launch traced here: 28.2 us
  Pallas kernels  27.6 us (98%)
  between operations  0.64 us (2%)
    pallas_call x1, Pallas kernels, local(): pl.pallas_call(kernel, out_shape=(jax.ShapeDtypeStruct(brick, F32), jax.S...  26.7 us
    pallas_call x1, Pallas kernels, local(): pl.pallas_call(emit, out_shape=(jax.ShapeDtypeStruct(brick, F32), jax.Sha...  0.89 us

profile of v9, /device:TPU:1, one launch (start us, length us, event | category | flops | bytes accessed | tf_op | source)
XLA Modules:
  0.0 28.2 jit_solution(10894889643089754400)
XLA Ops:
  0.6 26.7 %smooth.1 = (f32[16,24,256]{2,1,0:T(8,128)S(1)}, f32[16,24,256]{2,1,0:T(8,128)S(1)}) custom-call(f32[2,2,16,2,8,256]{5,4,3,2,1,0:T(8,128)} %bitcast.3, bf16[4,2,16,2,8,256]{5,4,3,2,1,0:T(8,128)(2,1)} %bitcast.4, s32[1,1,2]{2,1,0:T(1,128)} %bitcast.5), custom_call_target="tpu_custom_call" | custom-call | tf_op jit(solution)/shard_map/smooth/pallas_call | solution.py:650
  27.3 0.9 %emit.1 = (f32[16,24,256]{2,1,0:T(8,128)}, f32[16,24,256]{2,1,0:T(8,128)}) custom-call(f32[16,24,256]{2,1,0:T(8,128)S(1)} %get-tuple-element.4.x_ref, f32[16,24,256]{2,1,0:T(8,128)S(1)} %get-tuple-element.5.r_ref), custom_call_target="tpu_custom_call" | custom-call | tf_op jit(solution)/shard_map/emit/pallas_call | solution.py:726
